TPU v7x, 256 devices: a whole 4x4x8 slice. The times are simulated.
256 devices in a mesh: seq: 32 (over z_hi, x, core), tensor: 8 (over y, z_lo).
Axes of the slice: x: 4, y: 4, z: 8 (z_hi: 4, z_lo: 2; z = z_hi * 2 + z_lo), core: 2. Of those that a mesh axis runs over, the one named last changes fastest.
Arguments:
- tokens: bfloat16 [4096, 2048], P('seq'), may hold values from -6 to 6
- lengths: int32 [8], replicated, may hold values from 1 to 2048, 4096 in all
- page_table: int32 [256], replicated, may hold values from 0 to 255, each once
- attention_gain: float32 [2048], replicated, may hold values from 0.25 to 1.75
- query_weight: bfloat16 [2048, 2048], P(None, 'tensor')
- key_weight: bfloat16 [2048, 2048], P(None, 'tensor')
- value_weight: bfloat16 [2048, 2048], P(None, 'tensor'), may hold values from -0.125 to 0.125
- out_weight: bfloat16 [2048, 2048], P('tensor'), may hold values from -0.125 to 0.125
- expert_gain: float32 [2048], replicated, may hold values from 0.25 to 1.75
- router_weight: bfloat16 [2048, 64], replicated, may hold values from -0.03125 to 0.03125
- expert_ids: int32 [4096, 8], P('seq'), may hold values from 0 to 63, all different within a row; in each aligned block of 128 rows (0 to 127, 128 to 255, ...) at most 24 rows name the same one
- gate_weight: bfloat16 [64, 2048, 1024], P('seq', None, 'tensor'), may hold values from -0.125 to 0.125
- up_weight: bfloat16 [64, 2048, 1024], P('seq', None, 'tensor'), may hold values from -0.125 to 0.125
- down_weight: bfloat16 [64, 1024, 2048], P('seq', 'tensor'), may hold values from -6 to 6
Outputs:
- layer_out: bfloat16 [4096, 2048], P('seq')
- key_cache: bfloat16 [256, 16, 2048], P('seq', None, 'tensor')
- value_cache: bfloat16 [256, 16, 2048], P('seq', None, 'tensor')
Inputs may be any that keep to these rules, and one draw needn't show every extreme that they name: The 8 lengths sum to 4096; the longest is exactly 2048. `page_table`: every page number appears once. `expert_ids`: each token names 8 different experts; among the 128 tokens of one index of seq no expert is named more than 24 times, a bound that some block reaches.
All inputs are finite; a program needn't handle non-finite values.
Results may differ from a plain program's by a relative error of at most 0.023.
Values may be sent and summed in bfloat16 or wider, within the bound.
A program may use at most 128 MiB of HBM per device.

v0:
```python
import jax
import jax.numpy as jnp
from jax import lax
from jax.sharding import PartitionSpec as P

HEAD_DIM = 128
PAGE = 16


epsilon = 1e-05
rope_base = 10000.0


def rms_scale(matrix, scaling):
    mean_square = jnp.mean(matrix * matrix, axis=-1, keepdims=True)
    return matrix * lax.rsqrt(mean_square + epsilon) * scaling


def segment_info(lengths, places):
    starts = jnp.cumsum(lengths) - lengths
    inside = (places[:, None] >= starts[None, :]).astype(jnp.int32)
    segment = jnp.sum(inside, axis=1) - 1
    slot_ids = jnp.arange(starts.shape[0], dtype=jnp.int32)
    seg_start = jnp.sum(
        jnp.where(slot_ids[None, :] == segment[:, None], starts[None, :], 0), axis=1
    )
    return (segment, places - seg_start)


def rotate(matrix, position):
    half_dim = matrix.shape[-1] // 2
    frequency = jnp.exp(
        -jnp.log(rope_base) * jnp.arange(half_dim, dtype=jnp.float32) * (2.0 / matrix.shape[-1])
    )
    angles = position.astype(jnp.float32)[:, None] * frequency[None, :]
    cosine = jnp.cos(angles)[:, None, :]
    sine_part = jnp.sin(angles)[:, None, :]
    first_half = matrix[..., :half_dim]
    second = matrix[..., half_dim:]
    return jnp.concatenate(
        [first_half * cosine - second * sine_part, second * cosine + first_half * sine_part],
        axis=-1,
    )


def local(
    tokens,
    lengths,
    page_table,
    attention_gain,
    query_weight,
    key_weight,
    value_weight,
    out_weight,
    expert_gain,
    router_weight,
    expert_ids,
    gate_weight,
    up_weight,
    down_weight,
):
    row_count = tokens.shape[0]
    feature_count = tokens.shape[1]
    span_size = query_weight.shape[1]
    head_count = span_size // HEAD_DIM
    shard_id = lax.axis_index("seq")
    places = shard_id * row_count + jnp.arange(row_count, dtype=jnp.int32)
    segment, position = segment_info(lengths, places)
    stream = tokens.astype(jnp.float32)
    normed = rms_scale(stream, attention_gain).astype(jnp.bfloat16)
    queries = rotate(
        jnp.dot(normed, query_weight, preferred_element_type=jnp.float32).reshape(
            row_count, head_count, HEAD_DIM
        ),
        position,
    ).astype(jnp.bfloat16)
    key_rows = (
        rotate(
            jnp.dot(normed, key_weight, preferred_element_type=jnp.float32).reshape(
                row_count, head_count, HEAD_DIM
            ),
            position,
        )
        .astype(jnp.bfloat16)
        .reshape(row_count, span_size)
    )
    value_rows = jnp.dot(normed, value_weight, preferred_element_type=jnp.float32).astype(
        jnp.bfloat16
    )
    page_rows = row_count // PAGE
    my_pages = shard_id * page_rows + jnp.arange(page_rows, dtype=jnp.int32)
    owned = (page_table[None, :] == my_pages[:, None]).astype(jnp.bfloat16)
    score_scale = HEAD_DIM ** (-0.5)
    state = (
        jnp.full((head_count, row_count), -1e30, jnp.float32),
        jnp.zeros((head_count, row_count), jnp.float32),
        jnp.zeros((head_count, row_count, HEAD_DIM), jnp.float32),
    )
    key_piece = lax.all_gather(key_rows, "seq", axis=0, tiled=True)
    value_piece = lax.all_gather(value_rows, "seq", axis=0, tiled=True)
    piece_rows = key_piece.shape[0]
    key_pages = jnp.dot(
        owned,
        key_piece.reshape(piece_rows // PAGE, PAGE * span_size),
        preferred_element_type=jnp.float32,
    )
    value_pages = jnp.dot(
        owned,
        value_piece.reshape(piece_rows // PAGE, PAGE * span_size),
        preferred_element_type=jnp.float32,
    )
    row_peak, row_total, weighted = state
    piece_rows = key_piece.shape[0]
    key_places = jnp.arange(piece_rows, dtype=jnp.int32)
    key_segments, _ = segment_info(lengths, key_places)
    scores = (
        jnp.einsum(
            "qhd,khd->hqk",
            queries,
            key_piece.reshape(piece_rows, head_count, HEAD_DIM),
            preferred_element_type=jnp.float32,
        )
        * score_scale
    )
    allowed = (
        (segment[:, None] == key_segments[None, :]) & (key_places[None, :] <= places[:, None])
    )[None]
    new_peak = jnp.maximum(row_peak, jnp.max(jnp.where(allowed, scores, -1e30), axis=-1))
    raised = jnp.where(allowed, jnp.exp(scores - new_peak[:, :, None]), 0.0)
    row_total = jnp.sum(raised, axis=-1)
    weighted = jnp.einsum(
        "hqk,khd->hqd",
        raised.astype(jnp.bfloat16),
        value_piece.reshape(piece_rows, head_count, HEAD_DIM),
        preferred_element_type=jnp.float32,
    )
    state = (new_peak, row_total, weighted)
    state, key_pages, value_pages = (state, key_pages, value_pages)
    _, row_total, weighted = state
    attended = (
        jnp.transpose(weighted / row_total[:, :, None], (1, 0, 2))
        .reshape(row_count, span_size)
        .astype(jnp.bfloat16)
    )
    head_part = jnp.dot(attended, out_weight, preferred_element_type=jnp.float32)
    hidden = stream + lax.psum(head_part.astype(jnp.bfloat16), "tensor").astype(jnp.float32)
    moe_input = rms_scale(hidden, expert_gain).astype(jnp.bfloat16)
    expert_count = router_weight.shape[1]
    probability = jax.nn.softmax(
        jnp.dot(moe_input, router_weight, preferred_element_type=jnp.float32), axis=-1
    )
    expert_range = jnp.arange(expert_count, dtype=jnp.int32)
    chosen = jnp.sum(
        jnp.where(
            expert_ids[:, :, None] == expert_range[None, None, :], probability[:, None, :], 0.0
        ),
        axis=-1,
    )
    top_count = expert_ids.shape[1]
    flat_ids = expert_ids.reshape(-1)
    onehot = (flat_ids[:, None] == expert_range[None, :]).astype(jnp.int32)
    slot_rank = jnp.sum(jnp.cumsum(onehot, axis=0) * onehot, axis=1) - 1
    members = lax.axis_size("tensor")
    sources = lax.axis_size("seq")
    local_count = gate_weight.shape[0]
    base_room = row_count * top_count * 3 // (2 * expert_count)
    capacity = members * ((base_room + members - 1) // members)
    owners = jnp.arange(row_count * top_count, dtype=jnp.int32) // top_count
    slot_index = flat_ids * capacity + slot_rank
    row_table = (
        jnp.full((expert_count * capacity,), row_count, jnp.int32).at[slot_index].set(owners)
    )
    padded = jnp.concatenate([moe_input, jnp.zeros((1, feature_count), jnp.bfloat16)], axis=0)
    outgoing = padded[row_table].reshape(sources, local_count, capacity, feature_count)
    arrived = lax.all_to_all(outgoing, "seq", split_axis=0, concat_axis=0, tiled=True)
    gate_out = jnp.einsum(
        "sjnd,jdf->sjnf", arrived, gate_weight, preferred_element_type=jnp.float32
    )
    up_out = jnp.einsum("sjnd,jdf->sjnf", arrived, up_weight, preferred_element_type=jnp.float32)
    activation = (jax.nn.silu(gate_out) * up_out).astype(jnp.bfloat16)
    returned = lax.all_to_all(
        jnp.einsum(
            "sjnf,jfd->sjnd", activation, down_weight, preferred_element_type=jnp.float32
        ).astype(jnp.bfloat16),
        "seq",
        split_axis=0,
        concat_axis=0,
        tiled=True,
    )
    flat_rows = returned.reshape(expert_count * capacity, feature_count)
    picked = flat_rows[slot_index].astype(jnp.float32)
    mixture_part = jnp.sum(
        picked.reshape(row_count, top_count, feature_count) * chosen[:, :, None], axis=1
    )
    mixture = lax.psum(mixture_part.astype(jnp.bfloat16), "tensor").astype(jnp.float32)
    layer_out = (hidden + mixture).astype(jnp.bfloat16)
    key_cache = key_pages.reshape(page_rows, PAGE, span_size).astype(jnp.bfloat16)
    value_cache = value_pages.reshape(page_rows, PAGE, span_size).astype(jnp.bfloat16)
    return (layer_out, key_cache, value_cache)


def solution(mesh):
    return jax.shard_map(
        local,
        mesh=mesh,
        in_specs=(
            P("seq", None),
            P(),
            P(),
            P(),
            P(None, "tensor"),
            P(None, "tensor"),
            P(None, "tensor"),
            P("tensor", None),
            P(),
            P(),
            P("seq", None),
            P("seq", None, "tensor"),
            P("seq", None, "tensor"),
            P("seq", "tensor", None),
        ),
        out_specs=(P("seq", None), P("seq", None, "tensor"), P("seq", None, "tensor")),
        check_vma=False,
    )
```

profile of v0, /device:TPU:38, one launch (start us, length us, event | category | flops | bytes accessed | tf_op | source)
XLA Modules:
  0.0 648.2 jit_solution(417091453030510193)
XLA Ops:
  10.3 1.8 fusion.75
  12.2 1.8 fusion.77
  15.7 2.2 convolution_convert_fusion.3
  18.5 18.0 %reduce-window.20 = s32[64,8,128]{2,1,0:T(8,128)S(1)} reduce-window(s32[64,8,128]{2,1,0:T(8,128)S(1)} %fusion.52, s32[]{:T(128)} %constant.30.clone.1), window={size=1x1x128 pad=0_0x0_0x127_0}, to_apply=%region_9.10 | reduce-window | flops 8323072 | bytes 524292 | tf_op jit(solution)/shard_map/reduce-window.1
  37.8 33.4 %all-gather.3.cloned.1.call-done = bf16[4096,256]{0,1:T(8,128)(2,1)} async-done(((bf16[128,256]{0,1:T(8,128)(2,1)}), bf16[4096,256]{0,1:T(8,128)(2,1)}) %all-gather.3.cloned.1.call-update) | async-done | bytes 2097168 | tf_op jit(solution)/shard_map/all_gather | solution.py:99
  71.2 2.9 select_reduce_fusion
  74.1 1.9 copy-done.2
  77.1 50.2 %all-gather.5.cloned.1.call-done = bf16[4096,256]{1,0:T(8,128)(2,1)} async-done(((bf16[128,256]{1,0:T(8,128)(2,1)}), bf16[4096,256]{1,0:T(8,128)(2,1)}) %all-gather.5.cloned.1.call-update) | async-done | bytes 2097168 | tf_op jit(solution)/shard_map/all_gather | solution.py:100
  127.3 4.1 copy.95
  131.4 3.9 fusion.31
  136.5 4.3 scatter_custom_fusion
  140.9 72.8 %all-reduce.4.cloned.1.call-done = bf16[128,2048]{1,0:T(8,128)(2,1)} async-done(((bf16[128,2048]{1,0:T(8,128)(2,1)}), bf16[128,2048]{1,0:T(8,128)(2,1)}) %all-reduce.4.cloned.1.call-update) | async-done | bytes 524304 | tf_op jit(solution)/shard_map/psum | solution.py:146
  213.6 1.3 multiply_reduce_fusion
  214.9 1.3 multiply_convert_fusion
  217.1 7.1 %gather_fusion = bf16[1536,2048]{1,0:T(8,128)(2,1)} fusion(bf16[129,2048]{1,0:T(8,128)(2,1)S(1)} %concatenate.13, s32[2048]{0:T(1024)S(1)} %pad_clamp_fusion), kind=kCustom, calls=%fused_computation | custom fusion | bytes 12589056 | tf_op jit(solution)/shard_map/gather | solution.py:174
  224.1 151.6 %all_to_all.10 = bf16[32,2,24,2048]{3,2,1,0:T(8,128)(2,1)S(1)} all-to-all(bf16[32,2,24,2048]{3,2,1,0:T(8,128)(2,1)} %bitcast.85), channel_id=1, replica_groups=mesh['seq'=32,'tensor'=8] {'seq'}, dimensions={0} | all-to-all | bytes 12582912 | tf_op jit(solution)/shard_map/all_to_all | solution.py:175
  375.7 2.7 copy-done.5
  378.4 1.9 fusion.13
  380.3 8.9 %convert_bitcast_fusion = bf16[32,2,24,2048]{3,2,0,1:T(8,128)(2,1)} fusion(bf16[2,128,2048]{2,1,0:T(8,128)(2,1)S(1)} %copy-done, bf16[32,2,24,2048]{3,2,1,0:T(8,128)(2,1)} %copy-done.5, bf16[2,2048,128]{2,1,0:T(8,128)(2,1)S(1)} %copy-done.14, f32[32,2,24,128]{3,2,0,1:T(8,128)S(1)} %fusion.13), kind=kOutput, calls=%fused_computation.5 | convolution fusion | flops 1614938112 | bytes 15466496 | tf_op jit(solution)/shard_map/sjnf,jfd->sjnd/dot_general | solution.py:182
  389.2 6.6 %copy.84 = bf16[32,2,24,2048]{3,2,1,0:T(8,128)(2,1)} copy(bf16[32,2,24,2048]{3,2,0,1:T(8,128)(2,1)} %convert_bitcast_fusion) | data formatting | bytes 12582912 | tf_op jit(solution)/shard_map/convert_element_type | solution.py:184
  395.8 5.2 all-to-all-start.1
  401.3 3.3 copy.86
  404.6 2.4 reshape.277
  407.0 4.1 copy.87
  411.6 117.8 %all-to-all-done.1 = bf16[32,2,24,2048]{3,2,1,0:T(8,128)(2,1)} async-done(((bf16[32,2,24,2048]{3,2,1,0:T(8,128)(2,1)}), bf16[32,2,24,2048]{3,2,1,0:T(8,128)(2,1)}, u32[]{:S(2)}, u32[]{:S(2)}) %all-to-all-start.1) | async-done | bytes 6291488 | tf_op jit(solution)/shard_map/all_to_all | solution.py:181
  529.4 12.4 %gather_fusion.1 = bf16[1024,2048]{1,0:T(8,128)(2,1)} fusion(bf16[1536,2048]{1,0:T(8,128)(2,1)} %bitcast.22, s32[1024]{0:T(1024)S(1)} %broadcast_clamp_fusion), kind=kCustom, calls=%fused_computation.1 | custom fusion | bytes 8392704 | tf_op jit(solution)/shard_map/gather | solution.py:191
  541.8 7.5 %fusion = bf16[128,2048]{1,0:T(8,128)(2,1)} fusion(bf16[1024,2048]{1,0:T(8,128)(2,1)} %gather_fusion.1, f32[128,8]{1,0:T(8,128)S(1)} %copy.85), kind=kLoop, calls=%fused_computation.4 | loop fusion | flops 6029312 | bytes 4722688 | tf_op jit(solution)/shard_map/reduce_sum | solution.py:192
  549.3 2.2 convolution_convert_fusion.2
  552.2 2.4 reshape.278
  554.6 3.4 copy.88
  559.2 80.0 %all-reduce.6.cloned.1.call-done = bf16[128,2048]{1,0:T(8,128)(2,1)} async-done(((bf16[128,2048]{1,0:T(8,128)(2,1)}), bf16[128,2048]{1,0:T(8,128)(2,1)}) %all-reduce.6.cloned.1.call-update) | async-done | bytes 524304 | tf_op jit(solution)/shard_map/psum | solution.py:195
  639.2 2.4 add_convert_fusion
  (92 shorter events, 12.5 us)
Async XLA Ops:
  7.2 373.1 %copy-start = (bf16[2,128,2048]{2,1,0:T(8,128)(2,1)S(1)}, bf16[2,128,2048]{2,1,0:T(8,128)(2,1)}, u32[]{:S(2)}) copy-start(bf16[2,128,2048]{2,1,0:T(8,128)(2,1)} %param.27) | copy-start | bytes 3145732
  7.2 8.5 %copy-start.4 = (bf16[128,2048]{1,0:T(8,128)(2,1)S(1)}, bf16[128,2048]{1,0:T(8,128)(2,1)}, u32[]{:S(2)}) copy-start(bf16[128,2048]{1,0:T(8,128)(2,1)} %param.14) | copy-start | bytes 1572868
  7.2 8.5 %copy-start.15 = (f32[2048]{0:T(1024)S(1)}, f32[2048]{0:T(1024)}, u32[]{:S(2)}) copy-start(f32[2048]{0:T(1024)} %param.17) | copy-start | bytes 24580
  7.2 64.0 %all-gather.3.cloned.1.call-start = ((), (), s32[]{:S(2)}) async-start(), calls=%async_computation.2 | async-start | bytes 2162688 | tf_op jit(solution)/shard_map/all_gather | solution.py:99
  10.3 7.7 %copy-start.10 = (s32[128,8]{0,1:T(8,128)S(1)}, s32[128,8]{0,1:T(8,128)}, u32[]{:S(2)}) copy-start(s32[128,8]{0,1:T(8,128)} %param.24) | copy-start | bytes 12292
  15.6 111.7 %all-gather.5.cloned.1.call-start = ((), (), s32[]{:S(2)}) async-start(), calls=%async_computation.3 | async-start | bytes 2162688 | tf_op jit(solution)/shard_map/all_gather | solution.py:100
  17.9 195.7 %all-reduce.4.cloned.1.call-start = ((), (), s32[]{:S(2)}) async-start(), calls=%async_computation.4 | async-start | bytes 1048576 | tf_op jit(solution)/shard_map/psum | solution.py:146
  74.1 1.9 copy-start.2
  131.4 4.0 copy-start.8
  131.4 83.6 %copy-start.11 = (f32[2048]{0:T(1024)S(1)}, f32[2048]{0:T(1024)}, u32[]{:S(2)}) copy-start(f32[2048]{0:T(1024)} %param.22) | copy-start | bytes 24580
  216.2 0.8 copy-start.6
  224.1 154.2 %copy-start.13 = (bf16[2,2048,128]{2,1,0:T(8,128)(2,1)S(1)}, bf16[2,2048,128]{2,1,0:T(8,128)(2,1)}, u32[]{:S(2)}) copy-start(bf16[2,2048,128]{2,1,0:T(8,128)(2,1)} %param.25) | copy-start | bytes 3145732
  375.7 2.7 copy-start.5
  378.4 1.9 copy-start.14
  395.8 133.6 %all-to-all-start.1 = ((bf16[32,2,24,2048]{3,2,1,0:T(8,128)(2,1)}), bf16[32,2,24,2048]{3,2,1,0:T(8,128)(2,1)}, u32[]{:S(2)}, u32[]{:S(2)}) async-start(bf16[32,2,24,2048]{3,2,1,0:T(8,128)(2,1)} %copy.84), calls=%async_computation.1 | async-start | bytes 12582912 | tf_op jit(solution)/shard_map/all_to_all | solution.py:181
  401.0 238.2 %all-reduce.6.cloned.1.call-start = ((), (), s32[]{:S(2)}) async-start(), calls=%async_computation.5 | async-start | bytes 1048576 | tf_op jit(solution)/shard_map/psum | solution.py:195
  404.6 6.5 %copy-start.7 = (bf16[128,2048]{1,0:T(8,128)(2,1)S(1)}, bf16[128,2048]{1,0:T(8,128)(2,1)}, u32[]{:S(2)}) copy-start(bf16[128,2048]{1,0:T(8,128)(2,1)} %copy-done.6) | copy-start | bytes 1572868
  404.6 6.5 %copy-start.9 = (bf16[2048,64]{0,1:T(8,128)(2,1)S(1)}, bf16[2048,64]{0,1:T(8,128)(2,1)}, u32[]{:S(2)}) copy-start(bf16[2048,64]{0,1:T(8,128)(2,1)} %param.23) | copy-start | bytes 786436
  541.8 7.5 %copy-start.12 = (s32[256]{0:T(256)S(1)}, s32[256]{0:T(256)}, u32[]{:S(2)}) copy-start(s32[256]{0:T(256)} %param.16) | copy-start | bytes 3076
  541.8 10.4 %copy-start.3 = (bf16[4096,256]{1,0:T(8,128)(2,1)S(1)}, bf16[4096,256]{1,0:T(8,128)(2,1)}, u32[]{:S(2)}) copy-start(bf16[4096,256]{1,0:T(8,128)(2,1)} %all-gather.5.cloned.1.call-done) | copy-start | bytes 6291460
  554.6 87.1 %copy-start.1 = (bf16[2,128,2048]{2,1,0:T(8,128)(2,1)S(1)}, bf16[2,128,2048]{2,1,0:T(8,128)(2,1)}, u32[]{:S(2)}) copy-start(bf16[2,128,2048]{2,1,0:T(8,128)(2,1)} %param.27) | copy-start | bytes 3145732
Sparse Core Ops, SparseCore 0:
  15.7 55.4 all-gather.2
  74.3 52.9 all-gather.4
  136.6 76.9 all-reduce.3
  549.4 89.7 all-reduce.5
where the time goes:
time: 652 us; the launch traced here: 648 us
  waiting for transfers between devices  354 us (54%)
  blocking collectives  152 us (23%)
  local copies, waits for them, and re-layouts  58.9 us (9%)
  other arithmetic  36 us (6%)
  matrix products  27.7 us (4%)
  between operations  14.2 us (2%)
    all_to_all x1, blocking collectives, local(): lax.all_to_all(outgoing, 'seq', split_axis=0, concat_axis=0, tiled=True)  152 us
    all_to_all x1, waiting for transfers between devices, local(): lax.all_to_all(jnp.einsum('sjnf,jfd->sjnd', activation, down_weight, pref...  118 us
    psum x1, waiting for transfers between devices, local(): lax.psum(mixture_part.astype(jnp.bfloat16), 'tensor').astype(jnp.float32)  80 us
    psum x1, waiting for transfers between devices, local(): lax.psum(head_part.astype(jnp.bfloat16), 'tensor').astype(jnp.float32)  72.8 us
    all_gather x1, waiting for transfers between devices, local(): value_piece = lax.all_gather(value_rows, 'seq', axis=0, tiled=True)  50.2 us
    all_gather x1, waiting for transfers between devices, local(): key_piece = lax.all_gather(key_rows, 'seq', axis=0, tiled=True)  33.4 us
    another operation x5, other arithmetic  19.2 us
  transfers between devices with their start and end apart: 5, of which 5 were waited for; matrix products, arithmetic and copies ran while one was open for 8% of the time, Pallas kernels for 0%

commit v1 on v0

v1 whole, which is shorter than its diff:
```python
import functools

import jax
import jax.numpy as jnp
from jax import lax
from jax.experimental import pallas as pl
from jax.experimental.pallas import tpu as pltpu
from jax.sharding import PartitionSpec as P

HEAD_DIM = 128
PAGE = 16
RING = 4
MESH = pl.DeviceIdType.MESH

epsilon = 1e-05
rope_base = 10000.0


def place():
    seq = lax.axis_index("seq")
    tensor = lax.axis_index("tensor")
    return seq // 8, (seq // 2) % RING, seq % 2, tensor // 2, tensor % 2


def device(z, x, core, y, low):
    z, x, y = (z + RING) % RING, (x + RING) % RING, (y + RING) % RING
    return ((z * RING + x) * 2 + core, y * 2 + low)


def greet(peers):
    barrier = pltpu.get_barrier_semaphore()
    for peer in peers:
        pl.semaphore_signal(barrier, inc=1, device_id=peer, device_id_type=MESH)
    pl.semaphore_wait(barrier, len(peers))


class Wires:
    def __init__(self, send_sems, recv_sems):
        self.send_sems, self.recv_sems, self.copies = send_sems, recv_sems, []

    def push(self, source, target, peer):
        number = len(self.copies)
        copy = pltpu.make_async_remote_copy(
            src_ref=source,
            dst_ref=target,
            send_sem=self.send_sems.at[number],
            recv_sem=self.recv_sems.at[number],
            device_id=peer,
            device_id_type=MESH,
        )
        copy.start()
        self.copies.append(copy)
        return copy

    def drain(self):
        for copy in self.copies:
            copy.wait_send()


def spread(wires, view, half, near, far, mate, a, b):
    def wrap(v):
        return (v + RING) % RING

    mates = []

    def share(a_at, b_at):
        piece = view(a_at, b_at)
        mates.append(wires.push(piece, piece, mate))

    def across(a_at):
        piece = view(a_at, b)
        ahead = wires.push(piece, piece, far(1))
        back = wires.push(piece, piece, far(-1))
        share(a_at, b)
        return ahead, back

    own = view(a, b)
    ahead = wires.push(own, own, near(1))
    back = wires.push(own, own, near(-1))
    origins = [a, wrap(a - 1), wrap(a + 1), wrap(a + 2)]
    pairs = [across(origins[0])]
    ahead.wait_recv()
    part = half(origins[1], b, 0)
    ahead = wires.push(part, part, near(1))
    pairs.append(across(origins[1]))
    back.wait_recv()
    part = half(origins[2], b, 1)
    back = wires.push(part, part, near(-1))
    pairs.append(across(origins[2]))
    ahead.wait_recv()
    back.wait_recv()
    pairs.append(across(origins[3]))
    relays = []
    for number, (ahead, back) in enumerate(pairs):
        ahead.wait_recv()
        if number < 2:
            piece = view(origins[number], wrap(b - 1))
            relays.append(wires.push(piece, piece, far(1)))
        share(origins[number], wrap(b - 1))
        back.wait_recv()
        if number >= 2:
            piece = view(origins[number], wrap(b + 1))
            relays.append(wires.push(piece, piece, far(-1)))
        share(origins[number], wrap(b + 1))
    for number, relay in enumerate(relays):
        relay.wait_recv()
        share(origins[number], wrap(b + 2))
    for copy in mates:
        copy.wait_recv()


def gather_stream_kernel(mine, out, send_sems, recv_sems, local_sem):
    z, x, core, y, low = place()
    near = lambda step: device(z + step, x, core, y, low)
    far = lambda step: device(z, x + step, core, y, low)
    mate = device(z, x, 1 - core, y, low)
    greet([near(1), near(-1), far(1), far(-1), mate])
    local = pltpu.make_async_copy(mine, out.at[z, x, core], local_sem)
    local.start()
    local.wait()
    rows = mine.shape[0] // 2
    wires = Wires(send_sems, recv_sems)
    spread(
        wires,
        lambda a, b: out.at[a, b, core],
        lambda a, b, part: out.at[a, b, core, pl.ds(part * rows, rows)],
        near,
        far,
        mate,
        z,
        x,
    )
    wires.drain()


def gather_stream(mine):
    rows, columns = mine.shape
    copies = 4 + 8 + 4 + 16
    return pl.pallas_call(
        gather_stream_kernel,
        out_shape=jax.ShapeDtypeStruct((RING, RING, 2, rows, columns), mine.dtype),
        in_specs=[pl.BlockSpec(memory_space=pltpu.VMEM)],
        out_specs=pl.BlockSpec(memory_space=pl.ANY),
        scratch_shapes=[
            pltpu.SemaphoreType.DMA((copies,)),
            pltpu.SemaphoreType.DMA((copies,)),
            pltpu.SemaphoreType.DMA,
        ],
        compiler_params=pltpu.CompilerParams(collective_id=0, has_side_effects=True),
        name="gather_stream",
    )(mine).reshape(RING * RING * 2 * rows, columns)


def gather_all_kernel(mine, out, send_sems, recv_sems, local_sem):
    z, x, core, y, low = place()
    up = lambda step: device(z + step, x, core, y, low)
    twin = device(z, x, core, y, 1 - low)
    near = lambda step: device(z, x + step * (1 - core), core, y + step * core, low)
    far = lambda step: device(z, x + step * core, core, y + step * (1 - core), low)
    mate = device(z, x, 1 - core, y, low)
    greet([up(1), up(-1), twin, near(1), near(-1), far(1), far(-1), mate])
    wires = Wires(send_sems, recv_sems)
    local = pltpu.make_async_copy(mine, out.at[z, x, core, y, low], local_sem)
    local.start()
    copy = wires.push(mine, out.at[z, x, core, y, low], twin)
    local.wait()
    copy.wait_recv()
    both = out.at[z, x, core, y]
    ahead = wires.push(both, both, up(1))
    back = wires.push(both, both, up(-1))
    ahead.wait_recv()
    part = out.at[(z + 3) % RING, x, core, y, 0]
    ahead = wires.push(part, part, up(1))
    back.wait_recv()
    part = out.at[(z + 1) % RING, x, core, y, 1]
    back = wires.push(part, part, up(-1))
    ahead.wait_recv()
    back.wait_recv()

    def view(a, b):
        return out.at[:, a * (1 - core) + b * core, core, b * (1 - core) + a * core]

    def half(a, b, part):
        return out.at[
            pl.ds(part * 2, 2), a * (1 - core) + b * core, core, b * (1 - core) + a * core
        ]

    spread(
        wires, view, half, near, far, mate, x * (1 - core) + y * core, y * (1 - core) + x * core
    )
    wires.drain()


def gather_all(mine):
    rows, columns = mine.shape
    copies = 1 + 4 + 4 + 8 + 4 + 16
    return pl.pallas_call(
        gather_all_kernel,
        out_shape=jax.ShapeDtypeStruct((RING, RING, 2, RING, 2, rows, columns), mine.dtype),
        in_specs=[pl.BlockSpec(memory_space=pltpu.VMEM)],
        out_specs=pl.BlockSpec(memory_space=pl.ANY),
        scratch_shapes=[
            pltpu.SemaphoreType.DMA((copies,)),
            pltpu.SemaphoreType.DMA((copies,)),
            pltpu.SemaphoreType.DMA,
        ],
        compiler_params=pltpu.CompilerParams(collective_id=1, has_side_effects=True),
        name="gather_all",
    )(mine).reshape(RING * RING * 2 * RING * 2 * rows, columns)


def tensor_peers():
    seq, tensor = lax.axis_index("seq"), lax.axis_index("tensor")
    return [(seq, (tensor + step) % 8) for step in range(1, 8)]


def scatter_tensor_kernel(parts, out, landed, send_sems, recv_sems):
    tensor = lax.axis_index("tensor")
    peers = tensor_peers()
    greet(peers)
    wires = Wires(send_sems, recv_sems)
    for number, peer in enumerate(peers):
        wires.push(parts.at[peer[1]], landed.at[number], peer)
    total = parts[tensor].astype(jnp.float32)
    for number, copy in enumerate(wires.copies):
        copy.wait_recv()
        total = total + landed[number].astype(jnp.float32)
    out[...] = total
    wires.drain()


def scatter_tensor(parts):
    rows, columns = parts.shape[0] // 8, parts.shape[1]
    return pl.pallas_call(
        scatter_tensor_kernel,
        out_shape=jax.ShapeDtypeStruct((rows, columns), jnp.float32),
        in_specs=[pl.BlockSpec(memory_space=pltpu.VMEM)],
        out_specs=pl.BlockSpec(memory_space=pltpu.VMEM),
        scratch_shapes=[
            pltpu.VMEM((7, rows, columns), parts.dtype),
            pltpu.SemaphoreType.DMA((7,)),
            pltpu.SemaphoreType.DMA((7,)),
        ],
        compiler_params=pltpu.CompilerParams(collective_id=2, has_side_effects=True),
        name="scatter_tensor",
    )(parts.reshape(8, rows, columns))


def gather_tensor_kernel(mine, out, send_sems, recv_sems, local_sem):
    tensor = lax.axis_index("tensor")
    peers = tensor_peers()
    greet(peers)
    wires = Wires(send_sems, recv_sems)
    for peer in peers:
        wires.push(mine, out.at[tensor], peer)
    local = pltpu.make_async_copy(mine, out.at[tensor], local_sem)
    local.start()
    local.wait()
    for copy in wires.copies:
        copy.wait_recv()
    wires.drain()


def gather_tensor(mine):
    rows, columns = mine.shape
    return pl.pallas_call(
        gather_tensor_kernel,
        out_shape=jax.ShapeDtypeStruct((8, rows, columns), mine.dtype),
        in_specs=[pl.BlockSpec(memory_space=pltpu.VMEM)],
        out_specs=pl.BlockSpec(memory_space=pl.ANY),
        scratch_shapes=[
            pltpu.SemaphoreType.DMA((7,)),
            pltpu.SemaphoreType.DMA((7,)),
            pltpu.SemaphoreType.DMA,
        ],
        compiler_params=pltpu.CompilerParams(collective_id=3, has_side_effects=True),
        name="gather_tensor",
    )(mine).reshape(8 * rows, columns)


def scatter_all_kernel(
    parts, out, held, pair, far_relay, far_land, near_relay, near_land, up_relay, up_land, twin_land,
    send_sems, recv_sems, local_sems,
):
    z, x, core, y, low = place()
    up = lambda step: device(z + step, x, core, y, low)
    twin = device(z, x, core, y, 1 - low)
    near = lambda step: device(z, x + step * (1 - core), core, y + step * core, low)
    far = lambda step: device(z, x + step * core, core, y + step * (1 - core), low)
    mate = device(z, x, 1 - core, y, low)
    greet([up(1), up(-1), twin, near(1), near(-1), far(1), far(-1), mate])
    wires = Wires(send_sems, recv_sems)
    shifts = (2, 1, 3, 0)

    def piece(side, i, j):
        a = (x * (1 - side) + y * side + shifts[i]) % RING
        b = (y * (1 - side) + x * side + shifts[j]) % RING
        return parts.at[:, a * (1 - side) + b * side, side, b * (1 - side) + a * side]

    order = [(0, 0), (1, 0), (0, 1), (0, 2), (2, 0), (1, 1), (1, 2), (3, 0)]
    order += [(2, 1), (2, 2), (0, 3), (3, 1), (3, 2), (1, 3), (2, 3), (3, 3)]
    pairs, locals_ = {}, {}
    for i, j in order:
        k = i * RING + j
        pairs[k] = wires.push(piece(1 - core, i, j), pair.at[k], mate)
        locals_[k] = pltpu.make_async_copy(piece(core, i, j), held.at[k], local_sems.at[k])
        locals_[k].start()

    def add(target, first, count, sources):
        @pl.loop(0, count)
        def _(n):
            total = target[first + n].astype(jnp.float32)
            for source in sources:
                total = total + source[n].astype(jnp.float32)
            target[first + n] = total.astype(jnp.bfloat16)

    def meet(k):
        pairs[k].wait_recv()
        locals_[k].wait()

    relays, lands = {}, {}

    def opening(i):
        k = i * RING
        meet(k)
        add(held.at[k], 0, 4, [pair.at[k]])
        relays[i] = (
            wires.push(held.at[k, pl.ds(0, 2)], far_relay.at[i, 0], far(1)),
            wires.push(held.at[k, pl.ds(2, 2)], far_relay.at[i, 1], far(-1)),
        )

    def middle(i):
        for side, step in ((0, 1), (1, -1)):
            k = i * RING + 1 + side
            meet(k)
            add(held.at[k], 2 - 2 * side, 2, [pair.at[k, pl.ds(2 - 2 * side, 2)]])
            relays[i][side].wait_recv()
            add(held.at[k], 2 * side, 2, [pair.at[k, pl.ds(2 * side, 2)], far_relay.at[i, side]])
            lands[i, side] = wires.push(held.at[k], far_land.at[i, side], far(step))

    def closing(i):
        k = i * RING + 3
        meet(k)
        lands[i, 0].wait_recv()
        lands[i, 1].wait_recv()
        add(held.at[k], 0, 4, [pair.at[k], far_land.at[i, 0], far_land.at[i, 1]])

    opening(0)
    opening(1)
    middle(0)
    opening(2)
    middle(1)
    opening(3)
    middle(2)
    closing(0)
    near_copies = (
        wires.push(held.at[3, pl.ds(0, 2)], near_relay.at[0], near(1)),
        wires.push(held.at[3, pl.ds(2, 2)], near_relay.at[1], near(-1)),
    )
    middle(3)
    near_lands = []
    for side, step in ((0, 1), (1, -1)):
        closing(1 + side)
        near_copies[side].wait_recv()
        k = (1 + side) * RING + 3
        add(held.at[k], 2 * side, 2, [near_relay.at[side]])
        near_lands.append(wires.push(held.at[k], near_land.at[side], near(step)))
    closing(3)
    for copy in near_lands:
        copy.wait_recv()
    last = held.at[15]
    add(last, 0, 4, [near_land.at[0], near_land.at[1]])
    rows = out.shape[0]
    beyond = (z + 2) % RING
    up_copies = [
        wires.push(last.at[beyond, pl.ds(side * rows, rows)], up_relay.at[side], up(step))
        for side, step in ((0, 1), (1, -1))
    ]
    up_lands = []
    for side, step in ((0, 1), (1, -1)):
        up_copies[side].wait_recv()
        beside = (z + step + RING) % RING
        span = pl.ds(side * rows, rows)
        total = last[beside, span].astype(jnp.float32) + up_relay[side].astype(jnp.float32)
        last[beside, span] = total.astype(jnp.bfloat16)
        up_lands.append(wires.push(last.at[beside], up_land.at[side], up(step)))
    for copy in up_lands:
        copy.wait_recv()
    total = last[z].astype(jnp.float32)
    total = total + up_land[0].astype(jnp.float32) + up_land[1].astype(jnp.float32)
    last[z] = total.astype(jnp.bfloat16)
    other = pl.multiple_of((1 - low) * rows, rows)
    mine = pl.multiple_of(low * rows, rows)
    copy = wires.push(last.at[z, pl.ds(other, rows)], twin_land, twin)
    copy.wait_recv()
    out[...] = last[z, pl.ds(mine, rows)].astype(jnp.float32) + twin_land[...].astype(jnp.float32)
    wires.drain()


def scatter_all(parts):
    rows, columns = parts.shape[0] // (RING * RING * 2 * RING * 2), parts.shape[1]
    two = 2 * rows
    copies = 16 + 16 + 4 + 4 + 1
    grain = (RING, two, columns)
    halves = (2, two, columns)
    scratch = lambda *shape: pltpu.VMEM(shape, parts.dtype)
    return pl.pallas_call(
        scatter_all_kernel,
        out_shape=jax.ShapeDtypeStruct((rows, columns), jnp.float32),
        in_specs=[pl.BlockSpec(memory_space=pl.ANY)],
        out_specs=pl.BlockSpec(memory_space=pltpu.VMEM),
        scratch_shapes=[
            scratch(16, *grain),
            scratch(16, *grain),
            scratch(RING, 2, *halves),
            scratch(RING, 2, *grain),
            scratch(2, *halves),
            scratch(2, *grain),
            scratch(2, rows, columns),
            scratch(2, two, columns),
            scratch(rows, columns),
            pltpu.SemaphoreType.DMA((copies,)),
            pltpu.SemaphoreType.DMA((copies,)),
            pltpu.SemaphoreType.DMA((16,)),
        ],
        compiler_params=pltpu.CompilerParams(
            collective_id=4, has_side_effects=True, vmem_limit_bytes=40 * 1024 * 1024
        ),
        name="scatter_all",
    )(parts.reshape(RING, RING, 2, RING, two, columns))


def pages_kernel(blocks, kv, keys, values):
    columns = keys.shape[-1]
    keys[...] = kv[:, :, :columns]
    values[...] = kv[:, :, columns:]


def write_pages(kv, blocks, columns):
    count = blocks.shape[0]
    out = jax.ShapeDtypeStruct((count, PAGE, columns), kv.dtype)
    spec = pl.BlockSpec((1, PAGE, columns), lambda j, blocks: (j, 0, 0))
    return pl.pallas_call(
        pages_kernel,
        out_shape=(out, out),
        grid_spec=pltpu.PrefetchScalarGridSpec(
            num_scalar_prefetch=1,
            grid=(count,),
            in_specs=[pl.BlockSpec((1, PAGE, 2 * columns), lambda j, blocks: (blocks[j], 0, 0))],
            out_specs=(spec, spec),
        ),
        name="write_pages",
    )(blocks, kv.reshape(-1, PAGE, 2 * columns))


def rms_scale(matrix, scaling):
    mean_square = jnp.mean(matrix * matrix, axis=-1, keepdims=True)
    return matrix * lax.rsqrt(mean_square + epsilon) * scaling


def segment_info(lengths, places):
    starts = jnp.cumsum(lengths) - lengths
    inside = (places[:, None] >= starts[None, :]).astype(jnp.int32)
    segment = jnp.sum(inside, axis=1) - 1
    slot_ids = jnp.arange(starts.shape[0], dtype=jnp.int32)
    seg_start = jnp.sum(
        jnp.where(slot_ids[None, :] == segment[:, None], starts[None, :], 0), axis=1
    )
    return (segment, places - seg_start)


def rotate(matrix, position):
    half_dim = matrix.shape[-1] // 2
    frequency = jnp.exp(
        -jnp.log(rope_base) * jnp.arange(half_dim, dtype=jnp.float32) * (2.0 / matrix.shape[-1])
    )
    angles = position.astype(jnp.float32)[:, None] * frequency[None, :]
    cosine = jnp.cos(angles)[:, None, :]
    sine_part = jnp.sin(angles)[:, None, :]
    first_half = matrix[..., :half_dim]
    second = matrix[..., half_dim:]
    return jnp.concatenate(
        [first_half * cosine - second * sine_part, second * cosine + first_half * sine_part],
        axis=-1,
    )


def local(
    tokens,
    lengths,
    page_table,
    attention_gain,
    query_weight,
    key_weight,
    value_weight,
    out_weight,
    expert_gain,
    router_weight,
    expert_ids,
    gate_weight,
    up_weight,
    down_weight,
):
    row_count = tokens.shape[0]
    feature_count = tokens.shape[1]
    span_size = query_weight.shape[1]
    head_count = span_size // HEAD_DIM
    shard_id = lax.axis_index("seq")
    places = shard_id * row_count + jnp.arange(row_count, dtype=jnp.int32)
    segment, position = segment_info(lengths, places)
    stream = tokens.astype(jnp.float32)
    normed = rms_scale(stream, attention_gain).astype(jnp.bfloat16)

    def project(weight):
        return jnp.dot(normed, weight, preferred_element_type=jnp.float32)

    def turned(matrix):
        return rotate(matrix.reshape(row_count, head_count, HEAD_DIM), position).astype(
            jnp.bfloat16
        )

    key_rows = turned(project(key_weight)).reshape(row_count, span_size)
    value_rows = project(value_weight).astype(jnp.bfloat16)
    kv = gather_stream(jnp.concatenate([key_rows, value_rows], axis=1))
    queries = turned(project(query_weight))

    page_rows = row_count // PAGE
    my_pages = shard_id * page_rows + jnp.arange(page_rows, dtype=jnp.int32)
    block_ids = jnp.arange(page_table.shape[0], dtype=jnp.int32)
    blocks = jnp.sum(
        jnp.where(page_table[None, :] == my_pages[:, None], block_ids[None, :], 0), axis=1
    )
    key_cache, value_cache = write_pages(kv, blocks, span_size)

    piece_rows = kv.shape[0]
    key_places = jnp.arange(piece_rows, dtype=jnp.int32)
    key_segments, _ = segment_info(lengths, key_places)
    scores = jnp.einsum(
        "qhd,khd->hqk",
        queries,
        kv[:, :span_size].reshape(piece_rows, head_count, HEAD_DIM),
        preferred_element_type=jnp.float32,
    ) * (HEAD_DIM ** (-0.5))
    allowed = (
        (segment[:, None] == key_segments[None, :]) & (key_places[None, :] <= places[:, None])
    )[None]
    peak = jnp.max(jnp.where(allowed, scores, -1e30), axis=-1)
    raised = jnp.where(allowed, jnp.exp(scores - peak[:, :, None]), 0.0)
    row_total = jnp.sum(raised, axis=-1)
    weighted = jnp.einsum(
        "hqk,khd->hqd",
        raised.astype(jnp.bfloat16),
        kv[:, span_size:].reshape(piece_rows, head_count, HEAD_DIM),
        preferred_element_type=jnp.float32,
    )
    attended = (
        jnp.transpose(weighted / row_total[:, :, None], (1, 0, 2))
        .reshape(row_count, span_size)
        .astype(jnp.bfloat16)
    )
    head_part = jnp.dot(attended, out_weight, preferred_element_type=jnp.float32)

    member = lax.axis_index("tensor")
    own_rows = row_count // lax.axis_size("tensor")
    own_stream = lax.dynamic_slice_in_dim(tokens, member * own_rows, own_rows, 0)
    own_ids = lax.dynamic_slice_in_dim(expert_ids, member * own_rows, own_rows, 0)
    hidden = own_stream.astype(jnp.float32) + scatter_tensor(head_part.astype(jnp.bfloat16))
    moe_input = rms_scale(hidden, expert_gain).astype(jnp.bfloat16)
    expert_count = router_weight.shape[1]
    probability = jax.nn.softmax(
        jnp.dot(moe_input, router_weight, preferred_element_type=jnp.float32), axis=-1
    )
    expert_range = jnp.arange(expert_count, dtype=jnp.int32)
    named = jnp.any(own_ids[:, :, None] == expert_range[None, None, :], axis=1)
    share = jnp.where(named, probability, 0.0)
    share_high = share.astype(jnp.bfloat16)
    share_low = (share - share_high.astype(jnp.float32)).astype(jnp.bfloat16)

    everyone = gather_all(jnp.concatenate([moe_input, share_high, share_low], axis=1))
    rows = everyone[:, :feature_count]
    local_count = gate_weight.shape[0]
    part = None
    for number in range(local_count):
        expert = shard_id * local_count + number
        mine = (jnp.arange(2 * expert_count, dtype=jnp.int32) % expert_count == expert)[None, :]
        scale = jnp.sum(
            jnp.where(mine, everyone[:, feature_count:].astype(jnp.float32), 0.0),
            axis=1,
            keepdims=True,
        )
        gate_out = jnp.dot(rows, gate_weight[number], preferred_element_type=jnp.float32)
        up_out = jnp.dot(rows, up_weight[number], preferred_element_type=jnp.float32)
        activation = (jax.nn.silu(gate_out) * up_out * scale).astype(jnp.bfloat16)
        term = jnp.dot(activation, down_weight[number], preferred_element_type=jnp.float32)
        part = term if part is None else part + term
    mixture = scatter_all(part.astype(jnp.bfloat16))
    layer_out = gather_tensor((hidden + mixture).astype(jnp.bfloat16))
    return (layer_out, key_cache, value_cache)


def solution(mesh):
    return jax.shard_map(
        local,
        mesh=mesh,
        in_specs=(
            P("seq", None),
            P(),
            P(),
            P(),
            P(None, "tensor"),
            P(None, "tensor"),
            P(None, "tensor"),
            P("tensor", None),
            P(),
            P(),
            P("seq", None),
            P("seq", None, "tensor"),
            P("seq", None, "tensor"),
            P("seq", "tensor", None),
        ),
        out_specs=(P("seq", None), P("seq", None, "tensor"), P("seq", None, "tensor")),
        check_vma=False,
    )
```

time: 652 us -> 321 us (0.49)
  waiting for transfers between devices: 354 us -> 0 us
  Pallas kernels: 0 us -> 203 us
  blocking collectives: 152 us -> 0 us
  matrix products: 27.7 us -> 81.8 us
  local copies, waits for them, and re-layouts: 58.9 us -> 18 us
  other arithmetic: 36 us -> 14.6 us
  between operations: 14.2 us -> 0.94 us
    pallas_call x0 -> x6, Pallas kernels: none -> 203 us  [the longest x1 71.7 us: scatter_all(): pl.pallas_call(scatter_all_kernel, out_shape=jax.ShapeDtypeStruct((rows,...]
    psum x2 -> x0, waiting for transfers between devices: 153 us -> none  [the longest x1 80 us: local(): lax.psum(mixture_part.astype(jnp.bfloat16), 'tensor').astype(jnp.float32)]
    all_to_all x1 -> x0, blocking collectives: 152 us -> none  [local(): lax.all_to_all(outgoing, 'seq', split_axis=0, concat_axis=0, tiled=True)]
    all_to_all x1 -> x0, waiting for transfers between devices: 118 us -> none  [local(): lax.all_to_all(jnp.einsum('sjnf,jfd->sjnd', activation, down_weight, pref...]
    all_gather x2 -> x0, waiting for transfers between devices: 83.6 us -> none  [the longest x1 50.2 us: local(): value_piece = lax.all_gather(value_rows, 'seq', axis=0, tiled=True)]
    dot_general x9, matrix products: 26.3 us -> 80.4 us  [the longest x2 53 us: local(): jnp.dot(activation, down_weight[number], preferred_element_type=jnp.float32)]
    gather x2 -> x0, local copies, waits for them, and re-layouts: 19.5 us -> none  [the longest x1 12.4 us: local(): picked = flat_rows[slot_index].astype(jnp.float32)]
    another operation x6 -> x2, other arithmetic: 19.2 us -> 0.91 us
  transfers between devices with their start and end apart: 5 -> 0, of which waited for: 5 -> 0; matrix products, arithmetic and copies ran while one was open for 8% -> 0% of each run, Pallas kernels for 0% -> 0%
where the time goes in v1:
time: 321 us; the launch traced here: 318 us
  Pallas kernels  203 us (63%)
  matrix products  81.8 us (25%)
  local copies, waits for them, and re-layouts  18 us (6%)
  other arithmetic  14.6 us (5%)
    pallas_call x1, Pallas kernels, scatter_all(): pl.pallas_call(scatter_all_kernel, out_shape=jax.ShapeDtypeStruct((rows,...  71.7 us
    pallas_call x1, Pallas kernels, gather_all(): pl.pallas_call(gather_all_kernel, out_shape=jax.ShapeDtypeStruct((RING, R...  69 us
    dot_general x2, matrix products, local(): jnp.dot(activation, down_weight[number], preferred_element_type=jnp.float32)  53 us
    pallas_call x1, Pallas kernels, gather_stream(): pl.pallas_call(gather_stream_kernel, out_shape=jax.ShapeDtypeStruct((RING...  33.6 us
    dot_general x2, matrix products, local(): jnp.dot(rows, gate_weight[number], preferred_element_type=jnp.float32)  16.8 us
    pallas_call x1, Pallas kernels, scatter_tensor(): pl.pallas_call(scatter_tensor_kernel, out_shape=jax.ShapeDtypeStruct((row...  13.3 us
    pallas_call x1, Pallas kernels, gather_tensor(): pl.pallas_call(gather_tensor_kernel, out_shape=jax.ShapeDtypeStruct((8, r...  10.1 us
    unnamed x32, local copies, waits for them, and re-layouts  8.55 us

profile of v1, /device:TPU:38, one launch (start us, length us, event | category | flops | bytes accessed | tf_op | source)
XLA Modules:
  0.0 318.1 jit_solution(6529830461876500800)
XLA Ops:
  0.7 1.6 select_reduce_fusion.1.blocks
  2.3 0.8 reduce-window.9
  3.9 1.2 fusion.66
  5.2 0.8 constant_dynamic-slice_fusion
  6.3 1.8 convolution_convert_fusion.1
  8.3 1.8 fusion.108
  11.8 1.3 fusion.55
  13.1 33.6 %gather_stream.1 = bf16[4,4,2,128,512]{4,3,2,1,0:T(8,128)(2,1)} custom-call(bf16[128,512]{1,0:T(8,128)(2,1)} %pad_maximum_fusion.mine), custom_call_target="tpu_custom_call" | custom-call | tf_op jit(solution)/shard_map/gather_stream/pallas_call | solution.py:139
  46.8 5.0 %write_pages.1 = (bf16[8,16,256]{2,1,0:T(8,128)(2,1)}, bf16[8,16,256]{2,1,0:T(8,128)(2,1)}) custom-call(s32[8]{0:T(128)} %select_reduce_fusion.1.blocks, bf16[256,16,512]{2,1,0:T(8,128)(2,1)} %bitcast.59), custom_call_target="tpu_custom_call" | custom-call | tf_op jit(solution)/shard_map/write_pages/pallas_call | solution.py:443
  51.7 4.5 %fusion.112 = (bf16[4096,256]{1,0:T(8,128)(2,1)}, bf16[4096,256]{1,0:T(8,128)(2,1)}) fusion(bf16[4096,512]{1,0:T(8,128)(2,1)} %bitcast.60), kind=kLoop, calls=%fused_computation.120 | loop fusion | bytes 8388608 | tf_op jit(solution)/shard_map/slice | solution.py:541
  56.2 2.9 copy.47
  59.1 0.7 convolution_multiply_fusion
  60.2 1.7 fusion.115
  62.3 1.0 copy-done.3
  63.3 2.9 copy.40
  66.2 6.0 %fusion.63 = bf16[128,2,128]{0,2,1:T(8,128)(2,1)S(1)} fusion(bf16[4096,2,128]{0,2,1:T(8,128)(2,1)} %bitcast.63, f32[2,128,4096]{2,1,0:T(8,128)} %copy-done.5, pred[128,4096]{1,0:T(8,128)(4,1)} %fusion.55, f32[128,2]{0,1:T(2,128)S(1)} %bitcast.67), kind=kOutput, calls=%fused_computation.48 | convolution fusion | flops 272699648 | bytes 6882304 | tf_op jit(solution)/shard_map/hqk,khd->hqd/dot_general | solution.py:550
  72.3 1.1 convolution_convert_fusion
  73.4 13.3 %scatter_tensor.1 = f32[16,2048]{1,0:T(8,128)} custom-call(bf16[8,16,2048]{2,1,0:T(8,128)(2,1)} %bitcast.62), custom_call_target="tpu_custom_call" | custom-call | tf_op jit(solution)/shard_map/scatter_tensor/pallas_call | solution.py:234
  86.7 1.0 multiply_reduce_fusion
  87.8 1.0 multiply_convert_fusion
  89.4 0.7 concatenate.17.mine
  90.1 69.0 %gather_all.1 = bf16[4,4,2,4,2,16,2176]{6,5,4,3,2,1,0:T(8,128)(2,1)} custom-call(bf16[16,2176]{1,0:T(8,128)(2,1)} %concatenate.17.mine), custom_call_target="tpu_custom_call" | custom-call | tf_op jit(solution)/shard_map/gather_all/pallas_call | solution.py:197
  159.1 2.0 fusion.41
  161.1 9.6 %fusion.3 = f32[4096,128]{1,0:T(8,128)} fusion(bf16[4096,2176]{1,0:T(8,128)(2,1)} %bitcast.54, bf16[2,2048,128]{2,1,0:T(8,128)(2,1)S(1)} %copy-done.13), kind=kOutput, calls=%fused_computation.4 | convolution fusion | flops 2147483648 | bytes 19398656 | tf_op jit(solution)/shard_map/dot_general | solution.py:591
  170.7 2.0 copy-done.2
  172.7 7.2 %fusion.7 = f32[4096,128]{1,0:T(8,128)} fusion(bf16[4096,2176]{1,0:T(8,128)(2,1)S(1)} %bitcast.57, bf16[2,2048,128]{2,1,0:T(8,128)(2,1)} %param.25), kind=kOutput, calls=%fused_computation.8 | convolution fusion | flops 2147483648 | bytes 19398656 | tf_op jit(solution)/shard_map/dot_general | solution.py:591
  179.9 25.6 %fusion.36 = f32[4096,2048]{1,0:T(8,128)} fusion(bf16[4096,2176]{1,0:T(8,128)(2,1)} %bitcast.55, f32[4096,128]{1,0:T(8,128)} %fusion.7, f32[4096]{0:T(1024)S(1)} %get-tuple-element.8, bf16[2,128,2048]{2,1,0:T(8,128)(2,1)} %param.27, bf16[2,2048,128]{2,1,0:T(8,128)(2,1)S(1)} %copy-done.4), kind=kOutput, calls=%fused_computation.22 | convolution fusion | flops 4298637312 | bytes 53493760 | tf_op jit(solution)/shard_map/dot_general | solution.py:594
  205.5 27.4 %add_convert_fusion = bf16[4096,2048]{1,0:T(8,128)(2,1)} fusion(f32[4096,2048]{1,0:T(8,128)} %fusion.36, bf16[4096,2176]{1,0:T(8,128)(2,1)} %bitcast.56, f32[4096,128]{1,0:T(8,128)S(1)} %copy-done.6, f32[4096]{0:T(1024)S(1)} %get-tuple-element.7, bf16[2,128,2048]{2,1,0:T(8,128)(2,1)} %param.27, bf16[2,2048,128]{2,1,0:T(8,128)(2,1)S(1)} %copy-done.4), kind=kOutput, calls=%fused_computation.1 | convolution fusion | flops 4315414528 | bytes 70270976 | tf_op jit(solution)/shard_map/dot_general | solution.py:594
  232.9 71.7 %scatter_all.1 = f32[16,2048]{1,0:T(8,128)S(1)} custom-call(bf16[4,4,2,4,32,2048]{5,4,3,2,1,0:T(8,128)(2,1)} %bitcast.58), custom_call_target="tpu_custom_call" | custom-call | tf_op jit(solution)/shard_map/scatter_all/pallas_call | solution.py:407
  304.6 1.5 add_convert_fusion.1.mine
  306.1 10.1 %gather_tensor.1 = bf16[8,16,2048]{2,1,0:T(8,128)(2,1)} custom-call(bf16[16,2048]{1,0:T(8,128)(2,1)} %add_convert_fusion.1.mine), custom_call_target="tpu_custom_call" | custom-call | tf_op jit(solution)/shard_map/gather_tensor/pallas_call | solution.py:266
  316.2 1.9 copy.59
  (54 shorter events, 4.5 us)
Async XLA Ops:
  0.6 71.6 %copy-start = (bf16[256,2048]{1,0:T(8,128)(2,1)S(1)}, bf16[256,2048]{1,0:T(8,128)(2,1)}, u32[]{:S(2)}) copy-start(bf16[256,2048]{1,0:T(8,128)(2,1)} %param.21) | copy-start | bytes 3145732
  0.6 9.5 %copy-start.8 = (bf16[128,2048]{1,0:T(8,128)(2,1)S(1)}, bf16[128,2048]{1,0:T(8,128)(2,1)}, u32[]{:S(2)}) copy-start(bf16[128,2048]{1,0:T(8,128)(2,1)} %param.14) | copy-start | bytes 1572868
  0.7 9.5 %copy-start.14 = (f32[2048]{0:T(1024)S(1)}, f32[2048]{0:T(1024)}, u32[]{:S(2)}) copy-start(f32[2048]{0:T(1024)} %param.17) | copy-start | bytes 24580
  0.7 9.5 %copy-start.12 = (bf16[2048,256]{1,0:T(8,128)(2,1)S(1)}, bf16[2048,256]{1,0:T(8,128)(2,1)}, u32[]{:S(2)}) copy-start(bf16[2048,256]{1,0:T(8,128)(2,1)} %param.18) | copy-start | bytes 3145732
  59.1 1.0 copy-start.9
  60.2 2.1 copy-start.5
  60.2 3.1 copy-start.3
  66.2 21.6 %copy-start.11 = (f32[2048]{0:T(1024)S(1)}, f32[2048]{0:T(1024)}, u32[]{:S(2)}) copy-start(f32[2048]{0:T(1024)} %param.22) | copy-start | bytes 24580
  66.2 22.6 %copy-start.10 = (bf16[2048,64]{0,1:T(8,128)(2,1)S(1)}, bf16[2048,64]{0,1:T(8,128)(2,1)}, u32[]{:S(2)}) copy-start(bf16[2048,64]{0,1:T(8,128)(2,1)} %param.23) | copy-start | bytes 786436
  90.1 71.0 %copy-start.13 = (bf16[2,2048,128]{2,1,0:T(8,128)(2,1)S(1)}, bf16[2,2048,128]{2,1,0:T(8,128)(2,1)}, u32[]{:S(2)}) copy-start(bf16[2,2048,128]{2,1,0:T(8,128)(2,1)} %param.25) | copy-start | bytes 3145732
  161.1 11.6 %copy-start.2 = (bf16[4,4,2,4,2,16,2176]{6,5,4,3,2,1,0:T(8,128)(2,1)S(1)}, bf16[4,4,2,4,2,16,2176]{6,5,4,3,2,1,0:T(8,128)(2,1)}, u32[]{:S(2)}) copy-start(bf16[4,4,2,4,2,16,2176]{6,5,4,3,2,1,0:T(8,128)(2,1)} %gather_all.1) | copy-start | bytes 53477380
  172.7 7.2 %copy-start.4 = (bf16[2,2048,128]{2,1,0:T(8,128)(2,1)S(1)}, bf16[2,2048,128]{2,1,0:T(8,128)(2,1)}, u32[]{:S(2)}) copy-start(bf16[2,2048,128]{2,1,0:T(8,128)(2,1)} %param.26) | copy-start | bytes 3145732
  179.9 25.6 %copy-start.6 = (f32[4096,128]{1,0:T(8,128)S(1)}, f32[4096,128]{1,0:T(8,128)}, u32[]{:S(2)}) copy-start(f32[4096,128]{1,0:T(8,128)} %fusion.3) | copy-start | bytes 6291460
  232.9 71.7 %copy-start.7 = (f32[16,2048]{1,0:T(8,128)S(1)}, f32[16,2048]{1,0:T(8,128)}, u32[]{:S(2)}) copy-start(f32[16,2048]{1,0:T(8,128)} %scatter_tensor.1) | copy-start | bytes 393220
  232.9 85.2 %copy-start.1 = (bf16[256,2048]{1,0:T(8,128)(2,1)S(1)}, bf16[256,2048]{1,0:T(8,128)(2,1)}, u32[]{:S(2)}) copy-start(bf16[256,2048]{1,0:T(8,128)(2,1)} %param.21) | copy-start | bytes 3145732

commit v2 on v1

--- a/solution.py
+++ b/solution.py
@@ -151,64 +151,6 @@
     )(mine).reshape(RING * RING * 2 * rows, columns)
 
 
-def gather_all_kernel(mine, out, send_sems, recv_sems, local_sem):
-    z, x, core, y, low = place()
-    up = lambda step: device(z + step, x, core, y, low)
-    twin = device(z, x, core, y, 1 - low)
-    near = lambda step: device(z, x + step * (1 - core), core, y + step * core, low)
-    far = lambda step: device(z, x + step * core, core, y + step * (1 - core), low)
-    mate = device(z, x, 1 - core, y, low)
-    greet([up(1), up(-1), twin, near(1), near(-1), far(1), far(-1), mate])
-    wires = Wires(send_sems, recv_sems)
-    local = pltpu.make_async_copy(mine, out.at[z, x, core, y, low], local_sem)
-    local.start()
-    copy = wires.push(mine, out.at[z, x, core, y, low], twin)
-    local.wait()
-    copy.wait_recv()
-    both = out.at[z, x, core, y]
-    ahead = wires.push(both, both, up(1))
-    back = wires.push(both, both, up(-1))
-    ahead.wait_recv()
-    part = out.at[(z + 3) % RING, x, core, y, 0]
-    ahead = wires.push(part, part, up(1))
-    back.wait_recv()
-    part = out.at[(z + 1) % RING, x, core, y, 1]
-    back = wires.push(part, part, up(-1))
-    ahead.wait_recv()
-    back.wait_recv()
-
-    def view(a, b):
-        return out.at[:, a * (1 - core) + b * core, core, b * (1 - core) + a * core]
-
-    def half(a, b, part):
-        return out.at[
-            pl.ds(part * 2, 2), a * (1 - core) + b * core, core, b * (1 - core) + a * core
-        ]
-
-    spread(
-        wires, view, half, near, far, mate, x * (1 - core) + y * core, y * (1 - core) + x * core
-    )
-    wires.drain()
-
-
-def gather_all(mine):
-    rows, columns = mine.shape
-    copies = 1 + 4 + 4 + 8 + 4 + 16
-    return pl.pallas_call(
-        gather_all_kernel,
-        out_shape=jax.ShapeDtypeStruct((RING, RING, 2, RING, 2, rows, columns), mine.dtype),
-        in_specs=[pl.BlockSpec(memory_space=pltpu.VMEM)],
-        out_specs=pl.BlockSpec(memory_space=pl.ANY),
-        scratch_shapes=[
-            pltpu.SemaphoreType.DMA((copies,)),
-            pltpu.SemaphoreType.DMA((copies,)),
-            pltpu.SemaphoreType.DMA,
-        ],
-        compiler_params=pltpu.CompilerParams(collective_id=1, has_side_effects=True),
-        name="gather_all",
-    )(mine).reshape(RING * RING * 2 * RING * 2 * rows, columns)
-
-
 def tensor_peers():
     seq, tensor = lax.axis_index("seq"), lax.axis_index("tensor")
     return [(seq, (tensor + step) % 8) for step in range(1, 8)]
@@ -246,40 +188,9 @@
     )(parts.reshape(8, rows, columns))
 
 
-def gather_tensor_kernel(mine, out, send_sems, recv_sems, local_sem):
-    tensor = lax.axis_index("tensor")
-    peers = tensor_peers()
-    greet(peers)
-    wires = Wires(send_sems, recv_sems)
-    for peer in peers:
-        wires.push(mine, out.at[tensor], peer)
-    local = pltpu.make_async_copy(mine, out.at[tensor], local_sem)
-    local.start()
-    local.wait()
-    for copy in wires.copies:
-        copy.wait_recv()
-    wires.drain()
-
-
-def gather_tensor(mine):
-    rows, columns = mine.shape
-    return pl.pallas_call(
-        gather_tensor_kernel,
-        out_shape=jax.ShapeDtypeStruct((8, rows, columns), mine.dtype),
-        in_specs=[pl.BlockSpec(memory_space=pltpu.VMEM)],
-        out_specs=pl.BlockSpec(memory_space=pl.ANY),
-        scratch_shapes=[
-            pltpu.SemaphoreType.DMA((7,)),
-            pltpu.SemaphoreType.DMA((7,)),
-            pltpu.SemaphoreType.DMA,
-        ],
-        compiler_params=pltpu.CompilerParams(collective_id=3, has_side_effects=True),
-        name="gather_tensor",
-    )(mine).reshape(8 * rows, columns)
-
-
-def scatter_all_kernel(
-    parts, out, held, pair, far_relay, far_land, near_relay, near_land, up_relay, up_land, twin_land,
+def mixture_kernel(
+    mine, hidden, gate, up_part, down, out, rows_all, held, outbox, pair, near_relay, near_land,
+    far_relay, far_land, up_relay, up_land, twin_land, final, weight_in, weight_out,
     send_sems, recv_sems, local_sems,
 ):
     z, x, core, y, low = place()
@@ -288,23 +199,161 @@
     near = lambda step: device(z, x + step * (1 - core), core, y + step * core, low)
     far = lambda step: device(z, x + step * core, core, y + step * (1 - core), low)
     mate = device(z, x, 1 - core, y, low)
-    greet([up(1), up(-1), twin, near(1), near(-1), far(1), far(-1), mate])
+    a, b = x * (1 - core) + y * core, y * (1 - core) + x * core
+    peers = tensor_peers()
+    ring_y = [near(1), near(-1), far(1), far(-1)]
+    greet([up(1), up(-1), mate] + ring_y + peers)
     wires = Wires(send_sems, recv_sems)
-    shifts = (2, 1, 3, 0)
-
-    def piece(side, i, j):
-        a = (x * (1 - side) + y * side + shifts[i]) % RING
-        b = (y * (1 - side) + x * side + shifts[j]) % RING
-        return parts.at[:, a * (1 - side) + b * side, side, b * (1 - side) + a * side]
-
-    order = [(0, 0), (1, 0), (0, 1), (0, 2), (2, 0), (1, 1), (1, 2), (3, 0)]
-    order += [(2, 1), (2, 2), (0, 3), (3, 1), (3, 2), (1, 3), (2, 3), (3, 3)]
-    pairs, locals_ = {}, {}
-    for i, j in order:
-        k = i * RING + j
-        pairs[k] = wires.push(piece(1 - core, i, j), pair.at[k], mate)
-        locals_[k] = pltpu.make_async_copy(piece(core, i, j), held.at[k], local_sems.at[k])
-        locals_[k].start()
+    features, width = down.shape[2], gate.shape[2]
+    experts_here = gate.shape[0]
+    rows = mine.shape[0]
+
+    span = lambda member: pl.ds(pl.multiple_of(member * rows, rows), rows)
+    place_own = rows_all.at[z, x, core, y, span(low)]
+    loads = [pltpu.make_async_copy(mine, place_own, local_sems.at[0])]
+    for number in range(experts_here):
+        for kind, source in enumerate((gate, up_part)):
+            column = (kind * experts_here + number) * width
+            loads.append(
+                pltpu.make_async_copy(
+                    source.at[number],
+                    weight_in.at[:, pl.ds(column, width)],
+                    local_sems.at[len(loads)],
+                )
+            )
+        loads.append(
+            pltpu.make_async_copy(
+                down.at[number],
+                weight_out.at[pl.ds(number * width, width)],
+                local_sems.at[len(loads)],
+            )
+        )
+    for load in loads:
+        load.start()
+
+    def wrap(v):
+        return (v + RING) % RING
+
+    def view(side, a_at, b_at, first=0, count=RING):
+        return rows_all.at[
+            pl.ds(first, count),
+            a_at * (1 - side) + b_at * side,
+            side,
+            b_at * (1 - side) + a_at * side,
+        ]
+
+    copy = wires.push(mine, place_own, twin)
+    loads[0].wait()
+    copy.wait_recv()
+    both = rows_all.at[z, x, core, y]
+    ahead = wires.push(both, both, up(1))
+    back = wires.push(both, both, up(-1))
+    ahead.wait_recv()
+    piece = rows_all.at[wrap(z - 1), x, core, y, pl.ds(0, rows)]
+    ahead = wires.push(piece, piece, up(1))
+    back.wait_recv()
+    piece = rows_all.at[wrap(z + 1), x, core, y, pl.ds(rows, rows)]
+    back = wires.push(piece, piece, up(-1))
+    ahead.wait_recv()
+    back.wait_recv()
+
+    mates = []
+
+    def share(a_at, b_at):
+        piece = view(core, a_at, b_at)
+        mates.append(wires.push(piece, piece, mate))
+
+    def across(a_at):
+        piece = view(core, a_at, b)
+        ahead = wires.push(piece, piece, far(1))
+        back = wires.push(piece, piece, far(-1))
+        share(a_at, b)
+        return ahead, back
+
+    own = view(core, a, b)
+    ahead = wires.push(own, own, near(1))
+    back = wires.push(own, own, near(-1))
+    origins = [a, wrap(a - 1), wrap(a + 1), wrap(a + 2)]
+    pairs = [across(origins[0])]
+    ahead.wait_recv()
+    piece = view(core, origins[1], b, 0, 2)
+    ahead = wires.push(piece, piece, near(1))
+    pairs.append(across(origins[1]))
+    back.wait_recv()
+    piece = view(core, origins[2], b, 2, 2)
+    back = wires.push(piece, piece, near(-1))
+    pairs.append(across(origins[2]))
+    ahead.wait_recv()
+    back.wait_recv()
+    pairs.append(across(origins[3]))
+
+    relays = []
+
+    def onward(number):
+        ahead, back = pairs[number]
+        ahead.wait_recv()
+        if number < 2:
+            piece = view(core, origins[number], wrap(b - 1))
+            relays.append(wires.push(piece, piece, far(1)))
+        share(origins[number], wrap(b - 1))
+        back.wait_recv()
+        if number >= 2:
+            piece = view(core, origins[number], wrap(b + 1))
+            relays.append(wires.push(piece, piece, far(-1)))
+        share(origins[number], wrap(b + 1))
+
+    lines = (0, 3, 1, 2)
+    first_expert = lax.axis_index("seq") * experts_here
+    inner = experts_here * width
+
+    def experts(side, line, target):
+        a_side, b_side = x * (1 - side) + y * side, y * (1 - side) + x * side
+        b_at = (b_side + lines[line]) % RING
+
+        @pl.loop(0, RING)
+        def _(i):
+            a_at = (a_side + 2 + 3 * i) % RING
+            block = rows_all[
+                :, a_at * (1 - side) + b_at * side, side, b_at * (1 - side) + a_at * side
+            ]
+            block = block.reshape(RING * 2 * rows, block.shape[-1])
+            product = jnp.dot(
+                block[:, :features], weight_in[...], preferred_element_type=jnp.float32
+            )
+            shares = block[:, features:].astype(jnp.float32)
+            names = lax.broadcasted_iota(jnp.int32, shares.shape, 1) % (shares.shape[1] // 2)
+            scales = [
+                jnp.broadcast_to(
+                    jnp.sum(
+                        jnp.where(names == first_expert + number, shares, 0.0),
+                        axis=1,
+                        keepdims=True,
+                    ),
+                    (shares.shape[0], width),
+                )
+                for number in range(experts_here)
+            ]
+            gated = product[:, :inner]
+            active = gated / (1.0 + jnp.exp(-gated)) * product[:, inner:]
+            active = (active * jnp.concatenate(scales, axis=1)).astype(jnp.bfloat16)
+            term = jnp.dot(active, weight_out[...], preferred_element_type=jnp.float32)
+            target[line * RING + i] = term.astype(jnp.bfloat16).reshape(RING, 2 * rows, features)
+
+    exchanges = {}
+
+    def swap(line):
+        for i in (0, 1, 3, 2):
+            k = line * RING + i
+            exchanges[k] = wires.push(outbox.at[k], pair.at[k], mate)
+
+    def ours(line):
+        experts(core, line, held)
+
+    def theirs(line, numbers):
+        for number in numbers:
+            mates[number].wait_recv()
+        experts(1 - core, line, outbox)
+        swap(line)
 
     def add(target, first, count, sources):
         @pl.loop(0, count)
@@ -314,120 +363,157 @@
                 total = total + source[n].astype(jnp.float32)
             target[first + n] = total.astype(jnp.bfloat16)
 
-    def meet(k):
-        pairs[k].wait_recv()
-        locals_[k].wait()
-
-    relays, lands = {}, {}
-
-    def opening(i):
-        k = i * RING
-        meet(k)
-        add(held.at[k], 0, 4, [pair.at[k]])
-        relays[i] = (
-            wires.push(held.at[k, pl.ds(0, 2)], far_relay.at[i, 0], far(1)),
-            wires.push(held.at[k, pl.ds(2, 2)], far_relay.at[i, 1], far(-1)),
+    turns = {}
+    lands = {}
+
+    def opening(line):
+        k = line * RING
+        exchanges[k].wait_recv()
+        add(held.at[k], 0, RING, [pair.at[k]])
+        turns[line] = (
+            wires.push(held.at[k, pl.ds(0, 2)], near_relay.at[line, 0], near(1)),
+            wires.push(held.at[k, pl.ds(2, 2)], near_relay.at[line, 1], near(-1)),
         )
 
-    def middle(i):
-        for side, step in ((0, 1), (1, -1)):
-            k = i * RING + 1 + side
-            meet(k)
+    def middle(line):
+        for side, i, step in ((0, 1, 1), (1, 3, -1)):
+            k = line * RING + i
+            exchanges[k].wait_recv()
             add(held.at[k], 2 - 2 * side, 2, [pair.at[k, pl.ds(2 - 2 * side, 2)]])
-            relays[i][side].wait_recv()
-            add(held.at[k], 2 * side, 2, [pair.at[k, pl.ds(2 * side, 2)], far_relay.at[i, side]])
-            lands[i, side] = wires.push(held.at[k], far_land.at[i, side], far(step))
-
-    def closing(i):
-        k = i * RING + 3
-        meet(k)
-        lands[i, 0].wait_recv()
-        lands[i, 1].wait_recv()
-        add(held.at[k], 0, 4, [pair.at[k], far_land.at[i, 0], far_land.at[i, 1]])
-
+            turns[line][side].wait_recv()
+            add(held.at[k], 2 * side, 2, [pair.at[k, pl.ds(2 * side, 2)], near_relay.at[line, side]])
+            lands[line, side] = wires.push(held.at[k], near_land.at[line, side], near(step))
+
+    def closing(line):
+        k = line * RING + 2
+        exchanges[k].wait_recv()
+        lands[line, 0].wait_recv()
+        lands[line, 1].wait_recv()
+        add(held.at[k], 0, RING, [pair.at[k], near_land.at[line, 0], near_land.at[line, 1]])
+
+    def relayed(number):
+        relays[number].wait_recv()
+        share(origins[number], wrap(b + 2))
+
+    onward(0)
+    for load in loads[1:]:
+        load.wait()
+    ours(0)
+    onward(1)
+    theirs(0, (0, 1, 2, 3))
+    onward(2)
     opening(0)
+    onward(3)
+    ours(1)
+    middle(0)
+    relayed(0)
+    relayed(1)
+    theirs(1, (4, 6, 8, 10))
     opening(1)
-    middle(0)
+    closing(0)
+    ours(2)
+    relayed(2)
+    relayed(3)
+    middle(1)
+    theirs(2, (5, 7, 9, 11))
     opening(2)
-    middle(1)
+    closing(1)
+    ours(3)
+    middle(2)
+    theirs(3, (12, 13, 14, 15))
     opening(3)
-    middle(2)
-    closing(0)
-    near_copies = (
-        wires.push(held.at[3, pl.ds(0, 2)], near_relay.at[0], near(1)),
-        wires.push(held.at[3, pl.ds(2, 2)], near_relay.at[1], near(-1)),
-    )
+    closing(2)
     middle(3)
-    near_lands = []
-    for side, step in ((0, 1), (1, -1)):
-        closing(1 + side)
-        near_copies[side].wait_recv()
-        k = (1 + side) * RING + 3
-        add(held.at[k], 2 * side, 2, [near_relay.at[side]])
-        near_lands.append(wires.push(held.at[k], near_land.at[side], near(step)))
     closing(3)
-    for copy in near_lands:
+
+    line_sum = lambda line: held.at[line * RING + 2]
+    far_turns = (
+        wires.push(held.at[3 * RING + 2, pl.ds(0, 2)], far_relay.at[0], far(1)),
+        wires.push(held.at[3 * RING + 2, pl.ds(2, 2)], far_relay.at[1], far(-1)),
+    )
+    far_lands = []
+    for side, line, step in ((0, 2, 1), (1, 1, -1)):
+        far_turns[side].wait_recv()
+        add(line_sum(line), 2 * side, 2, [far_relay.at[side]])
+        far_lands.append(wires.push(line_sum(line), far_land.at[side], far(step)))
+    for copy in far_lands:
         copy.wait_recv()
-    last = held.at[15]
-    add(last, 0, 4, [near_land.at[0], near_land.at[1]])
-    rows = out.shape[0]
-    beyond = (z + 2) % RING
-    up_copies = [
+    last = line_sum(0)
+    add(last, 0, RING, [far_land.at[0], far_land.at[1]])
+
+    beyond = wrap(z + 2)
+    up_turns = [
         wires.push(last.at[beyond, pl.ds(side * rows, rows)], up_relay.at[side], up(step))
         for side, step in ((0, 1), (1, -1))
     ]
     up_lands = []
     for side, step in ((0, 1), (1, -1)):
-        up_copies[side].wait_recv()
-        beside = (z + step + RING) % RING
-        span = pl.ds(side * rows, rows)
-        total = last[beside, span].astype(jnp.float32) + up_relay[side].astype(jnp.float32)
-        last[beside, span] = total.astype(jnp.bfloat16)
+        up_turns[side].wait_recv()
+        beside = wrap(z + step)
+        part = pl.ds(side * rows, rows)
+        total = last[beside, part].astype(jnp.float32) + up_relay[side].astype(jnp.float32)
+        last[beside, part] = total.astype(jnp.bfloat16)
         up_lands.append(wires.push(last.at[beside], up_land.at[side], up(step)))
     for copy in up_lands:
         copy.wait_recv()
     total = last[z].astype(jnp.float32)
     total = total + up_land[0].astype(jnp.float32) + up_land[1].astype(jnp.float32)
     last[z] = total.astype(jnp.bfloat16)
-    other = pl.multiple_of((1 - low) * rows, rows)
-    mine = pl.multiple_of(low * rows, rows)
-    copy = wires.push(last.at[z, pl.ds(other, rows)], twin_land, twin)
+    copy = wires.push(last.at[z, span(1 - low)], twin_land, twin)
     copy.wait_recv()
-    out[...] = last[z, pl.ds(mine, rows)].astype(jnp.float32) + twin_land[...].astype(jnp.float32)
+    total = hidden[...] + last[z, span(low)].astype(jnp.float32)
+    final[...] = (total + twin_land[...].astype(jnp.float32)).astype(jnp.bfloat16)
+
+    local = pltpu.make_async_copy(final, out.at[y * 2 + low], local_sems.at[0])
+    local.start()
+    results = [wires.push(final, out.at[y * 2 + low], peer) for peer in peers]
+    local.wait()
+    for copy in results:
+        copy.wait_recv()
     wires.drain()
 
 
-def scatter_all(parts):
-    rows, columns = parts.shape[0] // (RING * RING * 2 * RING * 2), parts.shape[1]
+def mixture(mine, hidden, gate_weight, up_weight, down_weight):
+    rows, columns = mine.shape
+    features = hidden.shape[1]
+    here, _, width = gate_weight.shape
     two = 2 * rows
-    copies = 16 + 16 + 4 + 4 + 1
-    grain = (RING, two, columns)
-    halves = (2, two, columns)
-    scratch = lambda *shape: pltpu.VMEM(shape, parts.dtype)
+    kind = mine.dtype
+    copies = 1 + 4 + 4 + 8 + 4 + 16 + 16 + 16 + 4 + 4 + 1 + 7
+    grain = (RING, two, features)
+    halves = (2, two, features)
+    scratch = lambda *shape: pltpu.VMEM(shape, kind)
+    anywhere = pl.BlockSpec(memory_space=pl.ANY)
+    inside = pl.BlockSpec(memory_space=pltpu.VMEM)
     return pl.pallas_call(
-        scatter_all_kernel,
-        out_shape=jax.ShapeDtypeStruct((rows, columns), jnp.float32),
-        in_specs=[pl.BlockSpec(memory_space=pl.ANY)],
-        out_specs=pl.BlockSpec(memory_space=pltpu.VMEM),
+        mixture_kernel,
+        out_shape=jax.ShapeDtypeStruct((8, rows, features), kind),
+        in_specs=[inside, inside, anywhere, anywhere, anywhere],
+        out_specs=anywhere,
         scratch_shapes=[
+            scratch(RING, RING, 2, RING, two, columns),
+            scratch(16, *grain),
             scratch(16, *grain),
             scratch(16, *grain),
             scratch(RING, 2, *halves),
             scratch(RING, 2, *grain),
             scratch(2, *halves),
             scratch(2, *grain),
-            scratch(2, rows, columns),
-            scratch(2, two, columns),
-            scratch(rows, columns),
+            scratch(2, rows, features),
+            scratch(2, two, features),
+            scratch(rows, features),
+            scratch(rows, features),
+            scratch(features, 2 * here * width),
+            scratch(here * width, features),
             pltpu.SemaphoreType.DMA((copies,)),
             pltpu.SemaphoreType.DMA((copies,)),
-            pltpu.SemaphoreType.DMA((16,)),
+            pltpu.SemaphoreType.DMA((1 + 3 * here,)),
         ],
         compiler_params=pltpu.CompilerParams(
-            collective_id=4, has_side_effects=True, vmem_limit_bytes=40 * 1024 * 1024
+            collective_id=1, has_side_effects=True, vmem_limit_bytes=62 * 1024 * 1024
         ),
-        name="scatter_all",
-    )(parts.reshape(RING, RING, 2, RING, two, columns))
+        name="mixture",
+    )(mine, hidden, gate_weight, up_weight, down_weight).reshape(8 * rows, features)
 
 
 def pages_kernel(blocks, kv, keys, values):
@@ -576,25 +662,8 @@
     share_high = share.astype(jnp.bfloat16)
     share_low = (share - share_high.astype(jnp.float32)).astype(jnp.bfloat16)
 
-    everyone = gather_all(jnp.concatenate([moe_input, share_high, share_low], axis=1))
-    rows = everyone[:, :feature_count]
-    local_count = gate_weight.shape[0]
-    part = None
-    for number in range(local_count):
-        expert = shard_id * local_count + number
-        mine = (jnp.arange(2 * expert_count, dtype=jnp.int32) % expert_count == expert)[None, :]
-        scale = jnp.sum(
-            jnp.where(mine, everyone[:, feature_count:].astype(jnp.float32), 0.0),
-            axis=1,
-            keepdims=True,
-        )
-        gate_out = jnp.dot(rows, gate_weight[number], preferred_element_type=jnp.float32)
-        up_out = jnp.dot(rows, up_weight[number], preferred_element_type=jnp.float32)
-        activation = (jax.nn.silu(gate_out) * up_out * scale).astype(jnp.bfloat16)
-        term = jnp.dot(activation, down_weight[number], preferred_element_type=jnp.float32)
-        part = term if part is None else part + term
-    mixture = scatter_all(part.astype(jnp.bfloat16))
-    layer_out = gather_tensor((hidden + mixture).astype(jnp.bfloat16))
+    mine = jnp.concatenate([moe_input, share_high, share_low], axis=1)
+    layer_out = mixture(mine, hidden, gate_weight, up_weight, down_weight)
     return (layer_out, key_cache, value_cache)
 
 

time: 321 us -> 248 us (0.77)
  matrix products: 81.8 us -> 12.1 us
  other arithmetic: 14.6 us -> 10.2 us
  Pallas kernels: 203 us -> 207 us
    dot_general x4 -> x0, matrix products: 69.8 us -> none  [the longest x2 53 us: local(): jnp.dot(activation, down_weight[number], preferred_element_type=jnp.float32)]
    pallas_call x3 -> x1, Pallas kernels: 151 us -> 155 us  [mixture(): pl.pallas_call(mixture_kernel, out_shape=jax.ShapeDtypeStruct((8, rows, f...]
    unnamed x32 -> x22, local copies, waits for them, and re-layouts: 8.55 us -> 6.5 us
where the time goes in v2:
time: 248 us; the launch traced here: 246 us
  Pallas kernels  207 us (83%)
  local copies, waits for them, and re-layouts  15.9 us (6%)
  matrix products  12.1 us (5%)
  other arithmetic  10.2 us (4%)
    pallas_call x1, Pallas kernels, mixture(): pl.pallas_call(mixture_kernel, out_shape=jax.ShapeDtypeStruct((8, rows, f...  155 us
    pallas_call x1, Pallas kernels, gather_stream(): pl.pallas_call(gather_stream_kernel, out_shape=jax.ShapeDtypeStruct((RING...  33.6 us
    pallas_call x1, Pallas kernels, scatter_tensor(): pl.pallas_call(scatter_tensor_kernel, out_shape=jax.ShapeDtypeStruct((row...  13.2 us
    unnamed x22, local copies, waits for them, and re-layouts  6.5 us
    dot_general x1, matrix products, local(): jnp.einsum('hqk,khd->hqd', raised.astype(jnp.bfloat16), kv[:, span_size:]...  6.04 us
    pallas_call x1, Pallas kernels, write_pages(): pl.pallas_call(pages_kernel, out_shape=(out, out), grid_spec=pltpu.Prefet...  4.97 us

profile of v2, /device:TPU:38, one launch (start us, length us, event | category | flops | bytes accessed | tf_op | source)
XLA Modules:
  0.0 245.7 jit_solution(5864627599168162022)
XLA Ops:
  0.7 1.6 select_reduce_fusion.1.blocks
  2.3 0.8 reduce-window.9
  3.1 0.7 bitcast_subtract_fusion
  3.9 1.2 fusion.23
  5.2 0.8 constant_dynamic-slice_fusion
  6.1 0.1 convert_reduce_fusion
  6.3 1.8 convolution_convert_fusion.1
  8.0 0.3 multiply_cosine_fusion
  8.3 1.8 fusion.43
  10.2 0.4 fusion.45
  10.7 0.3 fusion.48
  11.2 0.7 pad_maximum_fusion.mine
  11.8 1.3 fusion.12
  13.1 33.6 %gather_stream.1 = bf16[4,4,2,128,512]{4,3,2,1,0:T(8,128)(2,1)} custom-call(bf16[128,512]{1,0:T(8,128)(2,1)} %pad_maximum_fusion.mine), custom_call_target="tpu_custom_call" | custom-call | tf_op jit(solution)/shard_map/gather_stream/pallas_call | solution.py:139
  46.7 5.0 %write_pages.1 = (bf16[8,16,256]{2,1,0:T(8,128)(2,1)}, bf16[8,16,256]{2,1,0:T(8,128)(2,1)}) custom-call(s32[8]{0:T(128)} %select_reduce_fusion.1.blocks, bf16[256,16,512]{2,1,0:T(8,128)(2,1)} %bitcast.31), custom_call_target="tpu_custom_call" | custom-call | tf_op jit(solution)/shard_map/write_pages/pallas_call | solution.py:529
  51.7 4.5 %fusion.47 = (bf16[4096,256]{1,0:T(8,128)(2,1)}, bf16[4096,256]{1,0:T(8,128)(2,1)}) fusion(bf16[4096,512]{1,0:T(8,128)(2,1)} %bitcast.32), kind=kLoop, calls=%fused_computation.68 | loop fusion | bytes 8388608 | tf_op jit(solution)/shard_map/slice | solution.py:627
  56.2 2.9 %copy.47 = bf16[4096,256]{0,1:T(8,128)(2,1)S(1)} copy(bf16[4096,256]{1,0:T(8,128)(2,1)} %get-tuple-element.9) | data formatting | bytes 4194304
  59.1 0.8 convolution_multiply_fusion
  59.9 0.3 copy-done.5
  60.1 1.7 fusion.50
  61.9 0.4 copy-done.2
  62.3 1.0 copy-done.1
  63.2 2.9 %copy.40 = bf16[4096,256]{0,1:T(8,128)(2,1)} copy(bf16[4096,256]{1,0:T(8,128)(2,1)S(1)} %copy-done.1) | data formatting | bytes 4194304 | tf_op jit(solution)/shard_map/slice | solution.py:639
  66.2 6.0 %fusion.20 = bf16[128,2,128]{0,2,1:T(8,128)(2,1)S(1)} fusion(bf16[4096,2,128]{0,2,1:T(8,128)(2,1)} %bitcast.35, f32[2,128,4096]{2,1,0:T(8,128)} %copy-done.2, pred[128,4096]{1,0:T(8,128)(4,1)} %fusion.12, f32[128,2]{0,1:T(2,128)S(1)} %bitcast.39), kind=kOutput, calls=%fused_computation.18 | convolution fusion | flops 272699648 | bytes 6882304 | tf_op jit(solution)/shard_map/hqk,khd->hqd/dot_general | solution.py:636
  72.2 1.1 convolution_convert_fusion
  73.3 13.2 %scatter_tensor.1 = f32[16,2048]{1,0:T(8,128)} custom-call(bf16[8,16,2048]{2,1,0:T(8,128)(2,1)} %bitcast.34), custom_call_target="tpu_custom_call" | custom-call | tf_op jit(solution)/shard_map/scatter_tensor/pallas_call | solution.py:176
  86.6 1.0 multiply_reduce_fusion
  87.7 0.3 fusion.51
  88.0 0.2 fusion.34
  88.3 0.7 concatenate.17.mine
  89.0 154.7 %mixture.1 = bf16[8,16,2048]{2,1,0:T(8,128)(2,1)} custom-call(bf16[16,2176]{1,0:T(8,128)(2,1)} %concatenate.17.mine, f32[16,2048]{1,0:T(8,128)} %copy-done.3, bf16[2,2048,128]{2,1,0:T(8,128)(2,1)} %gate.1, bf16[2,2048,128]{2,1,0:T(8,128)(2,1)} %up_part.1, bf16[2,128,2048]{2,1,0:T(8,128)(2,1)} %down.1), custom_call_target="tpu_custom_call" | custom-call | tf_op jit(solution)/shard_map/mixture/pallas_call | solution.py:488
  243.8 1.9 copy.59
  (35 shorter events, 0.9 us)
Async XLA Ops:
  0.6 71.6 %copy-start = (bf16[256,2048]{1,0:T(8,128)(2,1)S(1)}, bf16[256,2048]{1,0:T(8,128)(2,1)}, u32[]{:S(2)}) copy-start(bf16[256,2048]{1,0:T(8,128)(2,1)} %param.21) | copy-start | bytes 3145732
  0.6 9.5 %copy-start.4 = (bf16[128,2048]{1,0:T(8,128)(2,1)S(1)}, bf16[128,2048]{1,0:T(8,128)(2,1)}, u32[]{:S(2)}) copy-start(bf16[128,2048]{1,0:T(8,128)(2,1)} %param.14) | copy-start | bytes 1572868
  0.7 9.5 %copy-start.9 = (f32[2048]{0:T(1024)S(1)}, f32[2048]{0:T(1024)}, u32[]{:S(2)}) copy-start(f32[2048]{0:T(1024)} %param.17) | copy-start | bytes 24580
  0.7 9.5 %copy-start.8 = (bf16[2048,256]{1,0:T(8,128)(2,1)S(1)}, bf16[2048,256]{1,0:T(8,128)(2,1)}, u32[]{:S(2)}) copy-start(bf16[2048,256]{1,0:T(8,128)(2,1)} %param.18) | copy-start | bytes 3145732
  59.1 1.0 copy-start.5
  60.1 2.1 copy-start.2
  60.1 3.1 %copy-start.1 = (bf16[4096,256]{1,0:T(8,128)(2,1)S(1)}, bf16[4096,256]{1,0:T(8,128)(2,1)}, u32[]{:S(2)}) copy-start(bf16[4096,256]{1,0:T(8,128)(2,1)} %get-tuple-element.10) | copy-start | bytes 6291460
  66.2 21.5 %copy-start.7 = (f32[2048]{0:T(1024)S(1)}, f32[2048]{0:T(1024)}, u32[]{:S(2)}) copy-start(f32[2048]{0:T(1024)} %param.22) | copy-start | bytes 24580
  66.2 21.6 %copy-start.6 = (bf16[2048,64]{0,1:T(8,128)(2,1)S(1)}, bf16[2048,64]{0,1:T(8,128)(2,1)}, u32[]{:S(2)}) copy-start(bf16[2048,64]{0,1:T(8,128)(2,1)} %param.23) | copy-start | bytes 786436
  87.6 1.4 copy-start.3

commit v3 on v2

--- a/solution.py
+++ b/solution.py
@@ -10,6 +10,7 @@
 HEAD_DIM = 128
 PAGE = 16
 RING = 4
+BATCH = 2
 MESH = pl.DeviceIdType.MESH
 
 epsilon = 1e-05
@@ -57,136 +58,205 @@
             copy.wait_send()
 
 
-def spread(wires, view, half, near, far, mate, a, b):
+def tensor_peers():
+    seq, tensor = lax.axis_index("seq"), lax.axis_index("tensor")
+    return [(seq, (tensor + step) % 8) for step in range(1, 8)]
+
+
+def attend_kernel(
+    blocks, mine, normed, query_weight, cosine, sine, first, out_weight, own_stream,
+    hidden, key_pages, value_pages,
+    kv, parts, landed, queries, peak, total, weighted,
+    send_sems, recv_sems, local_sem,
+):
+    z, x, core, y, low = place()
+    near = lambda step: device(z + step, x, core, y, low)
+    far = lambda step: device(z, x + step, core, y, low)
+    mate = device(z, x, 1 - core, y, low)
+    peers = tensor_peers()
+    greet([near(1), near(-1), far(1), far(-1), mate] + peers)
+    wires = Wires(send_sems, recv_sems)
+    rows = normed.shape[0]
+    page_rows = rows // PAGE
+    span_size = query_weight.shape[1]
+    heads = span_size // HEAD_DIM
+
     def wrap(v):
         return (v + RING) % RING
 
+    local = pltpu.make_async_copy(mine, kv.at[core, x, z], local_sem)
+    local.start()
+    local.wait()
+
     mates = []
 
-    def share(a_at, b_at):
-        piece = view(a_at, b_at)
+    def share(z_at, x_at):
+        piece = kv.at[core, x_at, z_at]
         mates.append(wires.push(piece, piece, mate))
 
-    def across(a_at):
-        piece = view(a_at, b)
+    def across(z_at):
+        piece = kv.at[core, x, z_at]
         ahead = wires.push(piece, piece, far(1))
         back = wires.push(piece, piece, far(-1))
-        share(a_at, b)
+        share(z_at, x)
         return ahead, back
 
-    own = view(a, b)
+    half = page_rows // 2
+    own = kv.at[core, x, z]
     ahead = wires.push(own, own, near(1))
     back = wires.push(own, own, near(-1))
-    origins = [a, wrap(a - 1), wrap(a + 1), wrap(a + 2)]
+    origins = [z, wrap(z - 1), wrap(z + 1), wrap(z + 2)]
     pairs = [across(origins[0])]
+
+    product = jnp.dot(normed[...], query_weight[...], preferred_element_type=jnp.float32)
+    for head in range(heads):
+        one = product[:, head * HEAD_DIM : (head + 1) * HEAD_DIM]
+        one = one * cosine[...] + pltpu.roll(one, HEAD_DIM // 2, 1) * sine[...]
+        queries[head] = one.astype(jnp.bfloat16)
+    peak[...] = jnp.full(peak.shape, -1e30, jnp.float32)
+    total[...] = jnp.zeros(total.shape, jnp.float32)
+    weighted[...] = jnp.zeros(weighted.shape, jnp.float32)
+
     ahead.wait_recv()
-    part = half(origins[1], b, 0)
-    ahead = wires.push(part, part, near(1))
+    piece = kv.at[core, x, origins[1], pl.ds(0, half)]
+    ahead = wires.push(piece, piece, near(1))
     pairs.append(across(origins[1]))
     back.wait_recv()
-    part = half(origins[2], b, 1)
-    back = wires.push(part, part, near(-1))
+    piece = kv.at[core, x, origins[2], pl.ds(half, half)]
+    back = wires.push(piece, piece, near(-1))
     pairs.append(across(origins[2]))
     ahead.wait_recv()
     back.wait_recv()
     pairs.append(across(origins[3]))
     relays = []
-    for number, (ahead, back) in enumerate(pairs):
+
+    def onward(number):
+        ahead, back = pairs[number]
         ahead.wait_recv()
         if number < 2:
-            piece = view(origins[number], wrap(b - 1))
+            piece = kv.at[core, wrap(x - 1), origins[number]]
             relays.append(wires.push(piece, piece, far(1)))
-        share(origins[number], wrap(b - 1))
+        share(origins[number], wrap(x - 1))
         back.wait_recv()
         if number >= 2:
-            piece = view(origins[number], wrap(b + 1))
+            piece = kv.at[core, wrap(x + 1), origins[number]]
             relays.append(wires.push(piece, piece, far(-1)))
-        share(origins[number], wrap(b + 1))
-    for number, relay in enumerate(relays):
-        relay.wait_recv()
-        share(origins[number], wrap(b + 2))
-    for copy in mates:
+        share(origins[number], wrap(x + 1))
+
+    start_at = first[...]
+    here = lax.axis_index("seq") * rows + lax.broadcasted_iota(jnp.int32, (rows, 1), 0)
+    keys_in = RING * rows
+
+    def attend(side, x_at):
+        line = kv[side, x_at].reshape(keys_in, 2 * span_size)
+        column = lax.broadcasted_iota(jnp.int32, (1, keys_in), 1)
+        at = ((column // rows * RING + x_at) * 2 + side) * rows + column % rows
+        allowed = (at >= start_at) & (at <= here)
+        for head in range(heads):
+            keys = line[:, head * HEAD_DIM : (head + 1) * HEAD_DIM]
+            values = line[:, span_size + head * HEAD_DIM : span_size + (head + 1) * HEAD_DIM]
+            scores = lax.dot_general(
+                queries[head], keys, (((1,), (1,)), ((), ())), preferred_element_type=jnp.float32
+            ) * (HEAD_DIM ** (-0.5))
+            old = peak[head]
+            new = jnp.maximum(
+                old, jnp.max(jnp.where(allowed, scores, -1e30), axis=1, keepdims=True)
+            )
+            raised = jnp.where(allowed, jnp.exp(scores - new[:, :1]), 0.0)
+            keep = jnp.exp(old - new)
+            total[head] = total[head] * keep + jnp.sum(raised, axis=1, keepdims=True)
+            weighted[head] = weighted[head] * keep + jnp.dot(
+                raised.astype(jnp.bfloat16), values, preferred_element_type=jnp.float32
+            )
+            peak[head] = new
+
+    def arrived(numbers):
+        for number in numbers:
+            mates[number].wait_recv()
+
+    onward(0)
+    attend(core, x)
+    onward(1)
+    arrived((0, 1, 2, 3))
+    attend(1 - core, x)
+    onward(2)
+    onward(3)
+    attend(core, wrap(x - 1))
+    attend(core, wrap(x + 1))
+    relays[0].wait_recv()
+    share(origins[0], wrap(x + 2))
+    relays[1].wait_recv()
+    share(origins[1], wrap(x + 2))
+    arrived((4, 6, 8, 10))
+    attend(1 - core, wrap(x - 1))
+    relays[2].wait_recv()
+    share(origins[2], wrap(x + 2))
+    relays[3].wait_recv()
+    share(origins[3], wrap(x + 2))
+    arrived((5, 7, 9, 11))
+    attend(1 - core, wrap(x + 1))
+    attend(core, wrap(x + 2))
+    arrived((12, 13, 14, 15))
+    attend(1 - core, wrap(x + 2))
+
+    attended = jnp.concatenate(
+        [(weighted[head] / total[head]).astype(jnp.bfloat16) for head in range(heads)], axis=1
+    )
+    product = jnp.dot(attended, out_weight[...], preferred_element_type=jnp.float32)
+    parts[...] = product.astype(jnp.bfloat16).reshape(parts.shape)
+    sums = [
+        wires.push(parts.at[peer[1]], landed.at[number], peer) for number, peer in enumerate(peers)
+    ]
+
+    for j in range(key_pages.shape[0]):
+        block = blocks[j]
+        shard = block // page_rows
+        page = kv[shard % 2, (shard // 2) % RING, shard // (2 * RING), block % page_rows]
+        key_pages[j] = page[:, :span_size]
+        value_pages[j] = page[:, span_size:]
+
+    result = own_stream[...] + parts[lax.axis_index("tensor")].astype(jnp.float32)
+    for number, copy in enumerate(sums):
         copy.wait_recv()
-
-
-def gather_stream_kernel(mine, out, send_sems, recv_sems, local_sem):
-    z, x, core, y, low = place()
-    near = lambda step: device(z + step, x, core, y, low)
-    far = lambda step: device(z, x + step, core, y, low)
-    mate = device(z, x, 1 - core, y, low)
-    greet([near(1), near(-1), far(1), far(-1), mate])
-    local = pltpu.make_async_copy(mine, out.at[z, x, core], local_sem)
-    local.start()
-    local.wait()
-    rows = mine.shape[0] // 2
-    wires = Wires(send_sems, recv_sems)
-    spread(
-        wires,
-        lambda a, b: out.at[a, b, core],
-        lambda a, b, part: out.at[a, b, core, pl.ds(part * rows, rows)],
-        near,
-        far,
-        mate,
-        z,
-        x,
-    )
+        result = result + landed[number].astype(jnp.float32)
+    hidden[...] = result
     wires.drain()
 
 
-def gather_stream(mine):
+def attention(blocks, mine, normed, query_weight, cosine, sine, first, out_weight, own_stream):
     rows, columns = mine.shape
-    copies = 4 + 8 + 4 + 16
+    own_rows, features = own_stream.shape
+    heads = columns // (2 * HEAD_DIM)
+    page_rows = rows // PAGE
+    copies = 4 + 8 + 4 + 16 + 7
+    inside = pl.BlockSpec(memory_space=pltpu.VMEM)
+    pages = jax.ShapeDtypeStruct((page_rows, PAGE, columns // 2), mine.dtype)
+    state = pltpu.VMEM((heads, rows, HEAD_DIM), jnp.float32)
     return pl.pallas_call(
-        gather_stream_kernel,
-        out_shape=jax.ShapeDtypeStruct((RING, RING, 2, rows, columns), mine.dtype),
-        in_specs=[pl.BlockSpec(memory_space=pltpu.VMEM)],
-        out_specs=pl.BlockSpec(memory_space=pl.ANY),
+        attend_kernel,
+        out_shape=(jax.ShapeDtypeStruct((own_rows, features), jnp.float32), pages, pages),
+        in_specs=[pl.BlockSpec(memory_space=pltpu.SMEM)] + [inside] * 8,
+        out_specs=(inside, inside, inside),
         scratch_shapes=[
+            pltpu.VMEM((2, RING, RING, page_rows, PAGE, columns), mine.dtype),
+            pltpu.VMEM((8, own_rows, features), mine.dtype),
+            pltpu.VMEM((7, own_rows, features), mine.dtype),
+            pltpu.VMEM((heads, rows, HEAD_DIM), mine.dtype),
+            state,
+            state,
+            state,
             pltpu.SemaphoreType.DMA((copies,)),
             pltpu.SemaphoreType.DMA((copies,)),
             pltpu.SemaphoreType.DMA,
         ],
-        compiler_params=pltpu.CompilerParams(collective_id=0, has_side_effects=True),
-        name="gather_stream",
-    )(mine).reshape(RING * RING * 2 * rows, columns)
-
-
-def tensor_peers():
-    seq, tensor = lax.axis_index("seq"), lax.axis_index("tensor")
-    return [(seq, (tensor + step) % 8) for step in range(1, 8)]
-
-
-def scatter_tensor_kernel(parts, out, landed, send_sems, recv_sems):
-    tensor = lax.axis_index("tensor")
-    peers = tensor_peers()
-    greet(peers)
-    wires = Wires(send_sems, recv_sems)
-    for number, peer in enumerate(peers):
-        wires.push(parts.at[peer[1]], landed.at[number], peer)
-    total = parts[tensor].astype(jnp.float32)
-    for number, copy in enumerate(wires.copies):
-        copy.wait_recv()
-        total = total + landed[number].astype(jnp.float32)
-    out[...] = total
-    wires.drain()
-
-
-def scatter_tensor(parts):
-    rows, columns = parts.shape[0] // 8, parts.shape[1]
-    return pl.pallas_call(
-        scatter_tensor_kernel,
-        out_shape=jax.ShapeDtypeStruct((rows, columns), jnp.float32),
-        in_specs=[pl.BlockSpec(memory_space=pltpu.VMEM)],
-        out_specs=pl.BlockSpec(memory_space=pltpu.VMEM),
-        scratch_shapes=[
-            pltpu.VMEM((7, rows, columns), parts.dtype),
-            pltpu.SemaphoreType.DMA((7,)),
-            pltpu.SemaphoreType.DMA((7,)),
-        ],
-        compiler_params=pltpu.CompilerParams(collective_id=2, has_side_effects=True),
-        name="scatter_tensor",
-    )(parts.reshape(8, rows, columns))
-
+        compiler_params=pltpu.CompilerParams(
+            collective_id=0, has_side_effects=True, vmem_limit_bytes=40 * 1024 * 1024
+        ),
+        name="attention",
+    )(
+        blocks, mine.reshape(page_rows, PAGE, columns), normed, query_weight, cosine, sine, first,
+        out_weight, own_stream,
+    )
 
 def mixture_kernel(
     mine, hidden, gate, up_part, down, out, rows_all, held, outbox, pair, near_relay, near_land,
@@ -209,7 +279,7 @@
     rows = mine.shape[0]
 
     span = lambda member: pl.ds(pl.multiple_of(member * rows, rows), rows)
-    place_own = rows_all.at[z, x, core, y, span(low)]
+    place_own = rows_all.at[core, b, a, z, span(low)]
     loads = [pltpu.make_async_copy(mine, place_own, local_sems.at[0])]
     for number in range(experts_here):
         for kind, source in enumerate((gate, up_part)):
@@ -235,24 +305,19 @@
         return (v + RING) % RING
 
     def view(side, a_at, b_at, first=0, count=RING):
-        return rows_all.at[
-            pl.ds(first, count),
-            a_at * (1 - side) + b_at * side,
-            side,
-            b_at * (1 - side) + a_at * side,
-        ]
+        return rows_all.at[side, b_at, a_at, pl.ds(first, count)]
 
     copy = wires.push(mine, place_own, twin)
     loads[0].wait()
     copy.wait_recv()
-    both = rows_all.at[z, x, core, y]
+    both = rows_all.at[core, b, a, z]
     ahead = wires.push(both, both, up(1))
     back = wires.push(both, both, up(-1))
     ahead.wait_recv()
-    piece = rows_all.at[wrap(z - 1), x, core, y, pl.ds(0, rows)]
+    piece = rows_all.at[core, b, a, wrap(z - 1), pl.ds(0, rows)]
     ahead = wires.push(piece, piece, up(1))
     back.wait_recv()
-    piece = rows_all.at[wrap(z + 1), x, core, y, pl.ds(rows, rows)]
+    piece = rows_all.at[core, b, a, wrap(z + 1), pl.ds(rows, rows)]
     back = wires.push(piece, piece, up(-1))
     ahead.wait_recv()
     back.wait_recv()
@@ -307,16 +372,12 @@
     inner = experts_here * width
 
     def experts(side, line, target):
-        a_side, b_side = x * (1 - side) + y * side, y * (1 - side) + x * side
-        b_at = (b_side + lines[line]) % RING
-
-        @pl.loop(0, RING)
+        b_at = (y * (1 - side) + x * side + lines[line]) % RING
+
+        @pl.loop(0, RING // BATCH)
         def _(i):
-            a_at = (a_side + 2 + 3 * i) % RING
-            block = rows_all[
-                :, a_at * (1 - side) + b_at * side, side, b_at * (1 - side) + a_at * side
-            ]
-            block = block.reshape(RING * 2 * rows, block.shape[-1])
+            block = rows_all[side, b_at, pl.ds(i * BATCH, BATCH)]
+            block = block.reshape(BATCH * RING * 2 * rows, block.shape[-1])
             product = jnp.dot(
                 block[:, :features], weight_in[...], preferred_element_type=jnp.float32
             )
@@ -337,14 +398,16 @@
             active = gated / (1.0 + jnp.exp(-gated)) * product[:, inner:]
             active = (active * jnp.concatenate(scales, axis=1)).astype(jnp.bfloat16)
             term = jnp.dot(active, weight_out[...], preferred_element_type=jnp.float32)
-            target[line * RING + i] = term.astype(jnp.bfloat16).reshape(RING, 2 * rows, features)
+            target[line, pl.ds(i * BATCH, BATCH)] = term.astype(jnp.bfloat16).reshape(
+                BATCH, RING, 2 * rows, features
+            )
 
     exchanges = {}
 
     def swap(line):
-        for i in (0, 1, 3, 2):
-            k = line * RING + i
-            exchanges[k] = wires.push(outbox.at[k], pair.at[k], mate)
+        for step in (2, 1, 3, 0):
+            at = wrap(b + step)
+            exchanges[line, step] = wires.push(outbox.at[line, at], pair.at[line, at], mate)
 
     def ours(line):
         experts(core, line, held)
@@ -367,29 +430,29 @@
     lands = {}
 
     def opening(line):
-        k = line * RING
-        exchanges[k].wait_recv()
-        add(held.at[k], 0, RING, [pair.at[k]])
+        at = wrap(a + 2)
+        exchanges[line, 2].wait_recv()
+        add(held.at[line, at], 0, RING, [pair.at[line, at]])
         turns[line] = (
-            wires.push(held.at[k, pl.ds(0, 2)], near_relay.at[line, 0], near(1)),
-            wires.push(held.at[k, pl.ds(2, 2)], near_relay.at[line, 1], near(-1)),
+            wires.push(held.at[line, at, pl.ds(0, 2)], near_relay.at[line, 0], near(1)),
+            wires.push(held.at[line, at, pl.ds(2, 2)], near_relay.at[line, 1], near(-1)),
         )
 
     def middle(line):
-        for side, i, step in ((0, 1, 1), (1, 3, -1)):
-            k = line * RING + i
-            exchanges[k].wait_recv()
-            add(held.at[k], 2 - 2 * side, 2, [pair.at[k, pl.ds(2 - 2 * side, 2)]])
+        for side, step in ((0, 1), (1, 3)):
+            at = wrap(a + step)
+            exchanges[line, step].wait_recv()
+            piece, other = held.at[line, at], pair.at[line, at]
+            add(piece, 2 - 2 * side, 2, [other.at[pl.ds(2 - 2 * side, 2)]])
             turns[line][side].wait_recv()
-            add(held.at[k], 2 * side, 2, [pair.at[k, pl.ds(2 * side, 2)], near_relay.at[line, side]])
-            lands[line, side] = wires.push(held.at[k], near_land.at[line, side], near(step))
+            add(piece, 2 * side, 2, [other.at[pl.ds(2 * side, 2)], near_relay.at[line, side]])
+            lands[line, side] = wires.push(piece, near_land.at[line, side], near(1 - 2 * side))
 
     def closing(line):
-        k = line * RING + 2
-        exchanges[k].wait_recv()
+        exchanges[line, 0].wait_recv()
         lands[line, 0].wait_recv()
         lands[line, 1].wait_recv()
-        add(held.at[k], 0, RING, [pair.at[k], near_land.at[line, 0], near_land.at[line, 1]])
+        add(held.at[line, a], 0, RING, [pair.at[line, a], near_land.at[line, 0], near_land.at[line, 1]])
 
     def relayed(number):
         relays[number].wait_recv()
@@ -426,10 +489,10 @@
     middle(3)
     closing(3)
 
-    line_sum = lambda line: held.at[line * RING + 2]
+    line_sum = lambda line: held.at[line, a]
     far_turns = (
-        wires.push(held.at[3 * RING + 2, pl.ds(0, 2)], far_relay.at[0], far(1)),
-        wires.push(held.at[3 * RING + 2, pl.ds(2, 2)], far_relay.at[1], far(-1)),
+        wires.push(held.at[3, a, pl.ds(0, 2)], far_relay.at[0], far(1)),
+        wires.push(held.at[3, a, pl.ds(2, 2)], far_relay.at[1], far(-1)),
     )
     far_lands = []
     for side, line, step in ((0, 2, 1), (1, 1, -1)):
@@ -491,10 +554,10 @@
         in_specs=[inside, inside, anywhere, anywhere, anywhere],
         out_specs=anywhere,
         scratch_shapes=[
-            scratch(RING, RING, 2, RING, two, columns),
-            scratch(16, *grain),
-            scratch(16, *grain),
-            scratch(16, *grain),
+            scratch(2, RING, RING, RING, two, columns),
+            scratch(RING, RING, *grain),
+            scratch(RING, RING, *grain),
+            scratch(RING, RING, *grain),
             scratch(RING, 2, *halves),
             scratch(RING, 2, *grain),
             scratch(2, *halves),
@@ -514,29 +577,6 @@
         ),
         name="mixture",
     )(mine, hidden, gate_weight, up_weight, down_weight).reshape(8 * rows, features)
-
-
-def pages_kernel(blocks, kv, keys, values):
-    columns = keys.shape[-1]
-    keys[...] = kv[:, :, :columns]
-    values[...] = kv[:, :, columns:]
-
-
-def write_pages(kv, blocks, columns):
-    count = blocks.shape[0]
-    out = jax.ShapeDtypeStruct((count, PAGE, columns), kv.dtype)
-    spec = pl.BlockSpec((1, PAGE, columns), lambda j, blocks: (j, 0, 0))
-    return pl.pallas_call(
-        pages_kernel,
-        out_shape=(out, out),
-        grid_spec=pltpu.PrefetchScalarGridSpec(
-            num_scalar_prefetch=1,
-            grid=(count,),
-            in_specs=[pl.BlockSpec((1, PAGE, 2 * columns), lambda j, blocks: (blocks[j], 0, 0))],
-            out_specs=(spec, spec),
-        ),
-        name="write_pages",
-    )(blocks, kv.reshape(-1, PAGE, 2 * columns))
 
 
 def rms_scale(matrix, scaling):
@@ -607,8 +647,13 @@
 
     key_rows = turned(project(key_weight)).reshape(row_count, span_size)
     value_rows = project(value_weight).astype(jnp.bfloat16)
-    kv = gather_stream(jnp.concatenate([key_rows, value_rows], axis=1))
-    queries = turned(project(query_weight))
+    half_dim = HEAD_DIM // 2
+    frequency = jnp.exp(
+        -jnp.log(rope_base) * jnp.arange(half_dim, dtype=jnp.float32) * (2.0 / HEAD_DIM)
+    )
+    angles = position.astype(jnp.float32)[:, None] * frequency[None, :]
+    cosine = jnp.concatenate([jnp.cos(angles), jnp.cos(angles)], axis=1)
+    sine = jnp.concatenate([-jnp.sin(angles), jnp.sin(angles)], axis=1)
 
     page_rows = row_count // PAGE
     my_pages = shard_id * page_rows + jnp.arange(page_rows, dtype=jnp.int32)
@@ -616,41 +661,22 @@
     blocks = jnp.sum(
         jnp.where(page_table[None, :] == my_pages[:, None], block_ids[None, :], 0), axis=1
     )
-    key_cache, value_cache = write_pages(kv, blocks, span_size)
-
-    piece_rows = kv.shape[0]
-    key_places = jnp.arange(piece_rows, dtype=jnp.int32)
-    key_segments, _ = segment_info(lengths, key_places)
-    scores = jnp.einsum(
-        "qhd,khd->hqk",
-        queries,
-        kv[:, :span_size].reshape(piece_rows, head_count, HEAD_DIM),
-        preferred_element_type=jnp.float32,
-    ) * (HEAD_DIM ** (-0.5))
-    allowed = (
-        (segment[:, None] == key_segments[None, :]) & (key_places[None, :] <= places[:, None])
-    )[None]
-    peak = jnp.max(jnp.where(allowed, scores, -1e30), axis=-1)
-    raised = jnp.where(allowed, jnp.exp(scores - peak[:, :, None]), 0.0)
-    row_total = jnp.sum(raised, axis=-1)
-    weighted = jnp.einsum(
-        "hqk,khd->hqd",
-        raised.astype(jnp.bfloat16),
-        kv[:, span_size:].reshape(piece_rows, head_count, HEAD_DIM),
-        preferred_element_type=jnp.float32,
-    )
-    attended = (
-        jnp.transpose(weighted / row_total[:, :, None], (1, 0, 2))
-        .reshape(row_count, span_size)
-        .astype(jnp.bfloat16)
-    )
-    head_part = jnp.dot(attended, out_weight, preferred_element_type=jnp.float32)
 
     member = lax.axis_index("tensor")
     own_rows = row_count // lax.axis_size("tensor")
     own_stream = lax.dynamic_slice_in_dim(tokens, member * own_rows, own_rows, 0)
     own_ids = lax.dynamic_slice_in_dim(expert_ids, member * own_rows, own_rows, 0)
-    hidden = own_stream.astype(jnp.float32) + scatter_tensor(head_part.astype(jnp.bfloat16))
+    hidden, key_cache, value_cache = attention(
+        blocks,
+        jnp.concatenate([key_rows, value_rows], axis=1),
+        normed,
+        query_weight,
+        cosine,
+        sine,
+        (places - position)[:, None],
+        out_weight,
+        own_stream.astype(jnp.float32),
+    )
     moe_input = rms_scale(hidden, expert_gain).astype(jnp.bfloat16)
     expert_count = router_weight.shape[1]
     probability = jax.nn.softmax(

time: 248 us -> 216 us (0.87)
  matrix products: 12.1 us -> 0.9 us
  Pallas kernels: 207 us -> 197 us
  local copies, waits for them, and re-layouts: 15.9 us -> 9.75 us
  other arithmetic: 10.2 us -> 5.56 us
    pallas_call x3 -> x1, Pallas kernels: 51.8 us -> 43.2 us  [attention(): pl.pallas_call(attend_kernel, out_shape=(jax.ShapeDtypeStruct((own_rows,...]
    dot_general x3 -> x0, matrix products: 7.92 us -> none  [the longest x1 6.04 us: local(): jnp.einsum('hqk,khd->hqd', raised.astype(jnp.bfloat16), kv[:, span_size:]...]
    slice x3 -> x0, local copies, waits for them, and re-layouts: 7.72 us -> none  [the longest x1 4.48 us: local(): kv[:, :span_size].reshape(piece_rows, head_count, HEAD_DIM)]
    dot_general x3 -> x2, matrix products: 3.88 us -> 0.62 us  [project(): return jnp.dot(normed, weight, preferred_element_type=jnp.float32)]
    unnamed x22 -> x27, local copies, waits for them, and re-layouts: 6.5 us -> 8.64 us
where the time goes in v3:
time: 216 us; the launch traced here: 214 us
  Pallas kernels  197 us (91%)
  local copies, waits for them, and re-layouts  9.75 us (5%)
  other arithmetic  5.56 us (3%)
    pallas_call x1, Pallas kernels, mixture(): pl.pallas_call(mixture_kernel, out_shape=jax.ShapeDtypeStruct((8, rows, f...  154 us
    pallas_call x1, Pallas kernels, attention(): pl.pallas_call(attend_kernel, out_shape=(jax.ShapeDtypeStruct((own_rows,...  43.2 us
    unnamed x27, local copies, waits for them, and re-layouts  8.64 us

profile of v3, /device:TPU:38, one launch (start us, length us, event | category | flops | bytes accessed | tf_op | source)
XLA Modules:
  0.0 213.8 jit_solution(2873684368035432163)
XLA Ops:
  0.7 0.9 reduce-window.9
  1.6 0.7 bitcast_subtract_fusion
  2.3 0.1 convert_reduce_fusion
  2.4 0.1 select_reduce_fusion.1
  2.5 0.9 fusion.4
  3.4 1.2 fusion
  4.7 0.2 fusion.2.normed
  4.9 0.3 fusion.8
  5.3 0.3 subtract_convert_fusion
  5.6 0.2 pad_maximum_fusion.1
  5.8 0.3 copy-done.5
  6.1 0.3 convolution_convert_fusion
  6.5 0.8 copy-done.6
  7.3 0.1 pad_maximum_fusion.2
  7.4 0.1 copy.19.first
  7.6 0.7 copy-done.11
  8.2 0.2 select_reduce_fusion.blocks
  8.4 1.2 copy-done.2
  9.6 1.2 copy-done.3
  10.9 43.2 %attention.1 = (f32[16,2048]{1,0:T(8,128)S(1)}, bf16[8,16,256]{2,1,0:T(8,128)(2,1)S(1)}, bf16[8,16,256]{2,1,0:T(8,128)(2,1)S(1)}) custom-call(s32[8]{0:T(128)S(1)} %select_reduce_fusion.blocks, bf16[8,16,512]{2,1,0:T(8,128)(2,1)S(1)} %pad_maximum_fusion.mine, bf16[128,2048]{1,0:T(8,128)(2,1)S(1)} %fusion.2.normed, bf16[2048,256]{1,0:T(8,128)(2,1)S(1)} %copy-done.2, ...), custom_call_target="tpu_custom_call" | custom-call | tf_op jit(solution)/shard_map/attention/pallas_call | solution.py:235
  54.1 0.1 multiply_reduce_fusion
  54.3 0.4 copy-done.1
  54.7 0.4 copy-done.7
  55.0 0.3 fusion.7
  55.3 0.2 fusion.5
  55.5 0.5 copy-done.10
  56.2 0.1 fusion.3
  56.4 0.7 concatenate.24.mine
  57.1 153.6 %mixture.1 = bf16[8,16,2048]{2,1,0:T(8,128)(2,1)} custom-call(bf16[16,2176]{1,0:T(8,128)(2,1)} %concatenate.24.mine, f32[16,2048]{1,0:T(8,128)} %copy-done.1, bf16[2,2048,128]{2,1,0:T(8,128)(2,1)} %gate.1, bf16[2,2048,128]{2,1,0:T(8,128)(2,1)} %up_part.1, bf16[2,128,2048]{2,1,0:T(8,128)(2,1)} %down.1), custom_call_target="tpu_custom_call" | custom-call | tf_op jit(solution)/shard_map/mixture/pallas_call | solution.py:551
  210.7 1.9 copy.24
  212.6 0.6 copy.25
  213.2 0.6 copy.26
  (31 shorter events, 0.6 us)
Async XLA Ops:
  0.6 4.3 %copy-start = (bf16[2048,256]{1,0:T(8,128)(2,1)S(1)}, bf16[2048,256]{1,0:T(8,128)(2,1)}, u32[]{:S(2)}) copy-start(bf16[2048,256]{1,0:T(8,128)(2,1)} %param.19) | copy-start | bytes 3145732
  0.6 4.0 %copy-start.4 = (bf16[128,2048]{1,0:T(8,128)(2,1)S(1)}, bf16[128,2048]{1,0:T(8,128)(2,1)}, u32[]{:S(2)}) copy-start(bf16[128,2048]{1,0:T(8,128)(2,1)} %param.14) | copy-start | bytes 1572868
  3.4 1.3 copy-start.8
  4.9 1.2 copy-start.5
  6.4 0.8 copy-start.6
  7.5 0.7 copy-start.11
  8.4 1.2 copy-start.2
  9.6 1.2 copy-start.3
  10.8 43.3 %copy-start.9 = (f32[2048]{0:T(1024)S(1)}, f32[2048]{0:T(1024)}, u32[]{:S(2)}) copy-start(f32[2048]{0:T(1024)} %param.22) | copy-start | bytes 24580
  54.0 0.7 copy-start.1
  54.0 1.0 copy-start.7
  55.3 0.7 copy-start.10

commit v4 on v3

--- a/solution.py
+++ b/solution.py
@@ -310,17 +310,32 @@
     copy = wires.push(mine, place_own, twin)
     loads[0].wait()
     copy.wait_recv()
+    starts = [[], [], [], []]
+
+    def launch(z_at):
+        piece = rows_all.at[core, b, a, z_at]
+        for bundle, peer in zip(starts, (near(1), near(-1), far(1), far(-1))):
+            bundle.append(wires.push(piece, piece, peer))
+
+    def wait_all(bundle):
+        for copy in bundle:
+            copy.wait_recv()
+
     both = rows_all.at[core, b, a, z]
     ahead = wires.push(both, both, up(1))
     back = wires.push(both, both, up(-1))
+    launch(z)
     ahead.wait_recv()
     piece = rows_all.at[core, b, a, wrap(z - 1), pl.ds(0, rows)]
     ahead = wires.push(piece, piece, up(1))
+    launch(wrap(z - 1))
     back.wait_recv()
     piece = rows_all.at[core, b, a, wrap(z + 1), pl.ds(rows, rows)]
     back = wires.push(piece, piece, up(-1))
+    launch(wrap(z + 1))
     ahead.wait_recv()
     back.wait_recv()
+    launch(wrap(z + 2))
 
     mates = []
 
@@ -333,18 +348,16 @@
         ahead = wires.push(piece, piece, far(1))
         back = wires.push(piece, piece, far(-1))
         share(a_at, b)
-        return ahead, back
-
-    own = view(core, a, b)
-    ahead = wires.push(own, own, near(1))
-    back = wires.push(own, own, near(-1))
+        return [ahead], [back]
+
     origins = [a, wrap(a - 1), wrap(a + 1), wrap(a + 2)]
-    pairs = [across(origins[0])]
-    ahead.wait_recv()
+    share(a, b)
+    pairs = [(starts[2], starts[3])]
+    wait_all(starts[0])
     piece = view(core, origins[1], b, 0, 2)
     ahead = wires.push(piece, piece, near(1))
     pairs.append(across(origins[1]))
-    back.wait_recv()
+    wait_all(starts[1])
     piece = view(core, origins[2], b, 2, 2)
     back = wires.push(piece, piece, near(-1))
     pairs.append(across(origins[2]))
@@ -356,12 +369,12 @@
 
     def onward(number):
         ahead, back = pairs[number]
-        ahead.wait_recv()
+        wait_all(ahead)
         if number < 2:
             piece = view(core, origins[number], wrap(b - 1))
             relays.append(wires.push(piece, piece, far(1)))
         share(origins[number], wrap(b - 1))
-        back.wait_recv()
+        wait_all(back)
         if number >= 2:
             piece = view(core, origins[number], wrap(b + 1))
             relays.append(wires.push(piece, piece, far(-1)))
@@ -465,28 +478,28 @@
     onward(1)
     theirs(0, (0, 1, 2, 3))
     onward(2)
+    onward(3)
     opening(0)
-    onward(3)
     ours(1)
-    middle(0)
     relayed(0)
     relayed(1)
     theirs(1, (4, 6, 8, 10))
-    opening(1)
-    closing(0)
     ours(2)
     relayed(2)
     relayed(3)
-    middle(1)
+    opening(1)
+    middle(0)
     theirs(2, (5, 7, 9, 11))
+    ours(3)
     opening(2)
-    closing(1)
-    ours(3)
-    middle(2)
     theirs(3, (12, 13, 14, 15))
     opening(3)
+    middle(1)
+    middle(2)
+    middle(3)
+    closing(0)
+    closing(1)
     closing(2)
-    middle(3)
     closing(3)
 
     line_sum = lambda line: held.at[line, a]
@@ -494,29 +507,39 @@
         wires.push(held.at[3, a, pl.ds(0, 2)], far_relay.at[0], far(1)),
         wires.push(held.at[3, a, pl.ds(2, 2)], far_relay.at[1], far(-1)),
     )
-    far_lands = []
-    for side, line, step in ((0, 2, 1), (1, 1, -1)):
+    for side, line in ((0, 2), (1, 1)):
         far_turns[side].wait_recv()
         add(line_sum(line), 2 * side, 2, [far_relay.at[side]])
-        far_lands.append(wires.push(line_sum(line), far_land.at[side], far(step)))
-    for copy in far_lands:
-        copy.wait_recv()
+    far_lands = {}
+    for step in (2, 1, 3, 0):
+        at = wrap(z + step)
+        far_lands[step] = [
+            wires.push(line_sum(line).at[at], far_land.at[side, at], far(1 - 2 * side))
+            for side, line in ((0, 2), (1, 1))
+        ]
     last = line_sum(0)
-    add(last, 0, RING, [far_land.at[0], far_land.at[1]])
-
+
+    def finish(step):
+        at = wrap(z + step)
+        wait_all(far_lands[step])
+        add(last, at, 1, [far_land.at[0, pl.ds(at, 1)], far_land.at[1, pl.ds(at, 1)]])
+
+    finish(2)
     beyond = wrap(z + 2)
     up_turns = [
         wires.push(last.at[beyond, pl.ds(side * rows, rows)], up_relay.at[side], up(step))
         for side, step in ((0, 1), (1, -1))
     ]
     up_lands = []
-    for side, step in ((0, 1), (1, -1)):
+    for side, step in ((0, 1), (1, 3)):
+        finish(step)
         up_turns[side].wait_recv()
         beside = wrap(z + step)
         part = pl.ds(side * rows, rows)
         total = last[beside, part].astype(jnp.float32) + up_relay[side].astype(jnp.float32)
         last[beside, part] = total.astype(jnp.bfloat16)
-        up_lands.append(wires.push(last.at[beside], up_land.at[side], up(step)))
+        up_lands.append(wires.push(last.at[beside], up_land.at[side], up(1 - 2 * side)))
+    finish(0)
     for copy in up_lands:
         copy.wait_recv()
     total = last[z].astype(jnp.float32)
@@ -542,7 +565,7 @@
     here, _, width = gate_weight.shape
     two = 2 * rows
     kind = mine.dtype
-    copies = 1 + 4 + 4 + 8 + 4 + 16 + 16 + 16 + 4 + 4 + 1 + 7
+    copies = 1 + 4 + 16 + 2 + 6 + 4 + 16 + 16 + 16 + 10 + 4 + 1 + 7
     grain = (RING, two, features)
     halves = (2, two, features)
     scratch = lambda *shape: pltpu.VMEM(shape, kind)

time: 216 us -> 197 us (0.912)
  Pallas kernels: 197 us -> 179 us
    pallas_call x1, Pallas kernels: 154 us -> 136 us  [mixture(): pl.pallas_call(mixture_kernel, out_shape=jax.ShapeDtypeStruct((8, rows, f...]
where the time goes in v4:
time: 197 us; the launch traced here: 196 us
  Pallas kernels  179 us (91%)
  local copies, waits for them, and re-layouts  9.75 us (5%)
  other arithmetic  5.56 us (3%)
    pallas_call x1, Pallas kernels, mixture(): pl.pallas_call(mixture_kernel, out_shape=jax.ShapeDtypeStruct((8, rows, f...  136 us
    pallas_call x1, Pallas kernels, attention(): pl.pallas_call(attend_kernel, out_shape=(jax.ShapeDtypeStruct((own_rows,...  43.2 us
    unnamed x27, local copies, waits for them, and re-layouts  8.64 us

profile of v4, /device:TPU:38, one launch (start us, length us, event | category | flops | bytes accessed | tf_op | source)
XLA Modules:
  0.0 196.4 jit_solution(8462437666074873103)
XLA Ops:
  0.7 0.9 reduce-window.9
  1.6 0.7 bitcast_subtract_fusion
  2.3 0.1 convert_reduce_fusion
  2.4 0.1 select_reduce_fusion.1
  2.5 0.9 fusion.4
  3.4 1.2 fusion
  4.7 0.2 fusion.2.normed
  4.9 0.3 fusion.8
  5.3 0.3 subtract_convert_fusion
  5.6 0.2 pad_maximum_fusion.1
  5.8 0.3 copy-done.5
  6.1 0.3 convolution_convert_fusion
  6.5 0.8 copy-done.6
  7.3 0.1 pad_maximum_fusion.2
  7.4 0.1 copy.19.first
  7.6 0.7 copy-done.11
  8.2 0.2 select_reduce_fusion.blocks
  8.4 1.2 copy-done.2
  9.6 1.2 copy-done.3
  10.9 43.2 %attention.1 = (f32[16,2048]{1,0:T(8,128)S(1)}, bf16[8,16,256]{2,1,0:T(8,128)(2,1)S(1)}, bf16[8,16,256]{2,1,0:T(8,128)(2,1)S(1)}) custom-call(s32[8]{0:T(128)S(1)} %select_reduce_fusion.blocks, bf16[8,16,512]{2,1,0:T(8,128)(2,1)S(1)} %pad_maximum_fusion.mine, bf16[128,2048]{1,0:T(8,128)(2,1)S(1)} %fusion.2.normed, bf16[2048,256]{1,0:T(8,128)(2,1)S(1)} %copy-done.2, ...), custom_call_target="tpu_custom_call" | custom-call | tf_op jit(solution)/shard_map/attention/pallas_call | solution.py:235
  54.1 0.1 multiply_reduce_fusion
  54.3 0.4 copy-done.1
  54.7 0.4 copy-done.7
  55.0 0.3 fusion.7
  55.3 0.2 fusion.5
  55.5 0.5 copy-done.10
  56.2 0.1 fusion.3
  56.4 0.7 concatenate.24.mine
  57.1 136.2 %mixture.1 = bf16[8,16,2048]{2,1,0:T(8,128)(2,1)} custom-call(bf16[16,2176]{1,0:T(8,128)(2,1)} %concatenate.24.mine, f32[16,2048]{1,0:T(8,128)} %copy-done.1, bf16[2,2048,128]{2,1,0:T(8,128)(2,1)} %gate.1, bf16[2,2048,128]{2,1,0:T(8,128)(2,1)} %up_part.1, bf16[2,128,2048]{2,1,0:T(8,128)(2,1)} %down.1), custom_call_target="tpu_custom_call" | custom-call | tf_op jit(solution)/shard_map/mixture/pallas_call | solution.py:574
  193.3 1.9 copy.24
  195.2 0.6 copy.25
  195.8 0.6 copy.26
  (31 shorter events, 0.6 us)
Async XLA Ops:
  0.6 4.3 %copy-start = (bf16[2048,256]{1,0:T(8,128)(2,1)S(1)}, bf16[2048,256]{1,0:T(8,128)(2,1)}, u32[]{:S(2)}) copy-start(bf16[2048,256]{1,0:T(8,128)(2,1)} %param.19) | copy-start | bytes 3145732
  0.6 4.0 %copy-start.4 = (bf16[128,2048]{1,0:T(8,128)(2,1)S(1)}, bf16[128,2048]{1,0:T(8,128)(2,1)}, u32[]{:S(2)}) copy-start(bf16[128,2048]{1,0:T(8,128)(2,1)} %param.14) | copy-start | bytes 1572868
  3.4 1.3 copy-start.8
  4.9 1.2 copy-start.5
  6.4 0.8 copy-start.6
  7.5 0.7 copy-start.11
  8.4 1.2 copy-start.2
  9.6 1.2 copy-start.3
  10.8 43.3 %copy-start.9 = (f32[2048]{0:T(1024)S(1)}, f32[2048]{0:T(1024)}, u32[]{:S(2)}) copy-start(f32[2048]{0:T(1024)} %param.22) | copy-start | bytes 24580
  54.0 0.7 copy-start.1
  54.0 1.0 copy-start.7
  55.3 0.7 copy-start.10

commit v5 on v4

--- a/solution.py
+++ b/solution.py
@@ -64,10 +64,10 @@
 
 
 def attend_kernel(
-    blocks, mine, normed, query_weight, cosine, sine, first, out_weight, own_stream,
+    blocks, mine, normed, query_hbm, cosine, sine, first, out_hbm, own_stream,
     hidden, key_pages, value_pages,
-    kv, parts, landed, queries, peak, total, weighted,
-    send_sems, recv_sems, local_sem,
+    kv, parts, landed, queries, peak, total, weighted, query_weight, out_weight,
+    send_sems, recv_sems, local_sems,
 ):
     z, x, core, y, low = place()
     near = lambda step: device(z + step, x, core, y, low)
@@ -84,9 +84,14 @@
     def wrap(v):
         return (v + RING) % RING
 
-    local = pltpu.make_async_copy(mine, kv.at[core, x, z], local_sem)
-    local.start()
-    local.wait()
+    loads = [
+        pltpu.make_async_copy(source, target, local_sems.at[number])
+        for number, (source, target) in enumerate(
+            ((mine, kv.at[core, x, z]), (query_hbm, query_weight), (out_hbm, out_weight))
+        )
+    ]
+    for load in loads:
+        load.start()
 
     mates = []
 
@@ -103,10 +108,13 @@
 
     half = page_rows // 2
     own = kv.at[core, x, z]
-    ahead = wires.push(own, own, near(1))
-    back = wires.push(own, own, near(-1))
+    ahead = wires.push(mine, own, near(1))
+    back = wires.push(mine, own, near(-1))
     origins = [z, wrap(z - 1), wrap(z + 1), wrap(z + 2)]
-    pairs = [across(origins[0])]
+    pairs = [(wires.push(mine, own, far(1)), wires.push(mine, own, far(-1)))]
+    mates.append(wires.push(mine, own, mate))
+    for load in loads:
+        load.wait()
 
     product = jnp.dot(normed[...], query_weight[...], preferred_element_type=jnp.float32)
     for head in range(heads):
@@ -230,12 +238,16 @@
     page_rows = rows // PAGE
     copies = 4 + 8 + 4 + 16 + 7
     inside = pl.BlockSpec(memory_space=pltpu.VMEM)
+    anywhere = pl.BlockSpec(memory_space=pl.ANY)
     pages = jax.ShapeDtypeStruct((page_rows, PAGE, columns // 2), mine.dtype)
     state = pltpu.VMEM((heads, rows, HEAD_DIM), jnp.float32)
     return pl.pallas_call(
         attend_kernel,
         out_shape=(jax.ShapeDtypeStruct((own_rows, features), jnp.float32), pages, pages),
-        in_specs=[pl.BlockSpec(memory_space=pltpu.SMEM)] + [inside] * 8,
+        in_specs=[
+            pl.BlockSpec(memory_space=pltpu.SMEM),
+            inside, inside, anywhere, inside, inside, inside, anywhere, inside,
+        ],
         out_specs=(inside, inside, inside),
         scratch_shapes=[
             pltpu.VMEM((2, RING, RING, page_rows, PAGE, columns), mine.dtype),
@@ -245,12 +257,14 @@
             state,
             state,
             state,
+            pltpu.VMEM(query_weight.shape, query_weight.dtype),
+            pltpu.VMEM(out_weight.shape, out_weight.dtype),
             pltpu.SemaphoreType.DMA((copies,)),
             pltpu.SemaphoreType.DMA((copies,)),
-            pltpu.SemaphoreType.DMA,
+            pltpu.SemaphoreType.DMA((3,)),
         ],
         compiler_params=pltpu.CompilerParams(
-            collective_id=0, has_side_effects=True, vmem_limit_bytes=40 * 1024 * 1024
+            collective_id=0, has_side_effects=True, vmem_limit_bytes=62 * 1024 * 1024
         ),
         name="attention",
     )(
@@ -489,17 +503,14 @@
     relayed(3)
     opening(1)
     middle(0)
+    theirs(3, (12, 13, 14, 15))
+    ours(3)
+    opening(3)
     theirs(2, (5, 7, 9, 11))
-    ours(3)
     opening(2)
-    theirs(3, (12, 13, 14, 15))
-    opening(3)
     middle(1)
+    middle(3)
     middle(2)
-    middle(3)
-    closing(0)
-    closing(1)
-    closing(2)
     closing(3)
 
     line_sum = lambda line: held.at[line, a]
@@ -507,6 +518,9 @@
         wires.push(held.at[3, a, pl.ds(0, 2)], far_relay.at[0], far(1)),
         wires.push(held.at[3, a, pl.ds(2, 2)], far_relay.at[1], far(-1)),
     )
+    closing(2)
+    closing(1)
+    closing(0)
     for side, line in ((0, 2), (1, 1)):
         far_turns[side].wait_recv()
         add(line_sum(line), 2 * side, 2, [far_relay.at[side]])

time: 197 us -> 197 us (level)
  other arithmetic: 5.56 us -> 9.05 us
  local copies, waits for them, and re-layouts: 9.75 us -> 6.99 us
    unnamed x27 -> x29, local copies, waits for them, and re-layouts: 8.64 us -> 5.28 us
    pallas_call x1, Pallas kernels: 136 us -> 134 us  [mixture(): pl.pallas_call(mixture_kernel, out_shape=jax.ShapeDtypeStruct((8, rows, f...]
where the time goes in v5:
time: 197 us; the launch traced here: 196 us
  Pallas kernels  178 us (90%)
  other arithmetic  9.05 us (5%)
  local copies, waits for them, and re-layouts  6.99 us (4%)
    pallas_call x1, Pallas kernels, mixture(): pl.pallas_call(mixture_kernel, out_shape=jax.ShapeDtypeStruct((8, rows, f...  134 us
    pallas_call x1, Pallas kernels, attention(): pl.pallas_call(attend_kernel, out_shape=(jax.ShapeDtypeStruct((own_rows,...  44.6 us
    unnamed x29, local copies, waits for them, and re-layouts  5.28 us

profile of v5, /device:TPU:38, one launch (start us, length us, event | category | flops | bytes accessed | tf_op | source)
XLA Modules:
  0.0 196.3 jit_solution(11191127473520644344)
XLA Ops:
  0.7 0.9 reduce-window.9
  1.6 0.7 bitcast_subtract_fusion
  2.3 0.1 convert_reduce_fusion
  2.4 0.1 select_reduce_fusion.1
  2.5 0.9 fusion.4
  3.4 1.2 fusion
  4.7 0.2 fusion.2.normed
  4.9 0.3 fusion.8
  5.3 0.3 subtract_convert_fusion
  5.6 0.2 pad_maximum_fusion.1
  5.9 0.5 copy-done.4
  6.3 0.3 convolution_convert_fusion
  6.7 0.6 pad_maximum_fusion.mine
  7.3 0.2 copy-done.5
  7.5 0.8 pad_maximum_fusion.2
  8.2 0.7 dynamic-slice_convert_fusion.own_stream
  8.9 0.7 copy.19.first
  9.6 0.7 copy-done.12
  10.3 0.8 select_reduce_fusion.blocks
  11.1 44.6 %attention.1 = (f32[16,2048]{1,0:T(8,128)}, bf16[8,16,256]{2,1,0:T(8,128)(2,1)}, bf16[8,16,256]{2,1,0:T(8,128)(2,1)}) custom-call(s32[8]{0:T(128)} %select_reduce_fusion.blocks, bf16[8,16,512]{2,1,0:T(8,128)(2,1)} %pad_maximum_fusion.mine, bf16[128,2048]{1,0:T(8,128)(2,1)} %copy-done.1, bf16[2048,256]{1,0:T(8,128)(2,1)} %query_hbm.1, ...), custom_call_target="tpu_custom_call" | custom-call | tf_op jit(solution)/shard_map/attention/pallas_call | solution.py:244
  55.7 1.1 multiply_reduce_fusion
  56.8 0.1 multiply_convert_fusion
  56.9 0.3 fusion.7
  57.2 0.2 fusion.5
  57.4 0.5 copy-done.11
  58.0 0.1 fusion.3
  58.2 0.7 concatenate.24.mine
  58.9 133.9 %mixture.1 = bf16[8,16,2048]{2,1,0:T(8,128)(2,1)} custom-call(bf16[16,2176]{1,0:T(8,128)(2,1)} %concatenate.24.mine, f32[16,2048]{1,0:T(8,128)} %get-tuple-element.6.hidden, bf16[2,2048,128]{2,1,0:T(8,128)(2,1)} %gate.1, bf16[2,2048,128]{2,1,0:T(8,128)(2,1)} %up_part.1, bf16[2,128,2048]{2,1,0:T(8,128)(2,1)} %down.1), custom_call_target="tpu_custom_call" | custom-call | tf_op jit(solution)/shard_map/mixture/pallas_call | solution.py:588
  192.9 1.9 copy.24
  194.8 0.6 copy.25
  195.4 0.2 copy-done.7
  195.6 0.6 copy.26
  (33 shorter events, 0.5 us)
Async XLA Ops:
  0.6 4.3 %copy-start = (bf16[2048,256]{1,0:T(8,128)(2,1)S(1)}, bf16[2048,256]{1,0:T(8,128)(2,1)}, u32[]{:S(2)}) copy-start(bf16[2048,256]{1,0:T(8,128)(2,1)} %param.19) | copy-start | bytes 3145732
  0.6 4.0 %copy-start.2 = (bf16[128,2048]{1,0:T(8,128)(2,1)S(1)}, bf16[128,2048]{1,0:T(8,128)(2,1)}, u32[]{:S(2)}) copy-start(bf16[128,2048]{1,0:T(8,128)(2,1)} %param.14) | copy-start | bytes 1572868
  3.4 1.3 copy-start.9
  4.9 1.0 copy-start.1
  4.9 1.4 copy-start.4
  6.6 0.8 copy-start.5
  9.6 0.7 copy-start.12
  11.1 45.7 %copy-start.10 = (f32[2048]{0:T(1024)S(1)}, f32[2048]{0:T(1024)}, u32[]{:S(2)}) copy-start(f32[2048]{0:T(1024)} %param.22) | copy-start | bytes 24580
  11.1 45.8 %copy-start.6 = (bf16[2048,64]{0,1:T(8,128)(2,1)S(1)}, bf16[2048,64]{0,1:T(8,128)(2,1)}, u32[]{:S(2)}) copy-start(bf16[2048,64]{0,1:T(8,128)(2,1)} %param.23) | copy-start | bytes 786436
  55.6 1.1 copy-start.3
  57.2 0.7 copy-start.11
  192.8 1.9 copy-start.8
  194.8 0.9 copy-start.7

commit v6 on v4

--- a/solution.py
+++ b/solution.py
@@ -489,17 +489,14 @@
     relayed(3)
     opening(1)
     middle(0)
+    theirs(3, (12, 13, 14, 15))
+    ours(3)
+    opening(3)
     theirs(2, (5, 7, 9, 11))
-    ours(3)
     opening(2)
-    theirs(3, (12, 13, 14, 15))
-    opening(3)
     middle(1)
+    middle(3)
     middle(2)
-    middle(3)
-    closing(0)
-    closing(1)
-    closing(2)
     closing(3)
 
     line_sum = lambda line: held.at[line, a]
@@ -507,6 +504,9 @@
         wires.push(held.at[3, a, pl.ds(0, 2)], far_relay.at[0], far(1)),
         wires.push(held.at[3, a, pl.ds(2, 2)], far_relay.at[1], far(-1)),
     )
+    closing(2)
+    closing(1)
+    closing(0)
     for side, line in ((0, 2), (1, 1)):
         far_turns[side].wait_recv()
         add(line_sum(line), 2 * side, 2, [far_relay.at[side]])

time: 197 us -> 195 us (0.990)
  Pallas kernels: 179 us -> 177 us
    pallas_call x1, Pallas kernels: 136 us -> 134 us  [mixture(): pl.pallas_call(mixture_kernel, out_shape=jax.ShapeDtypeStruct((8, rows, f...]
where the time goes in v6:
time: 195 us; the launch traced here: 194 us
  Pallas kernels  177 us (91%)
  local copies, waits for them, and re-layouts  9.75 us (5%)
  other arithmetic  5.56 us (3%)
    pallas_call x1, Pallas kernels, mixture(): pl.pallas_call(mixture_kernel, out_shape=jax.ShapeDtypeStruct((8, rows, f...  134 us
    pallas_call x1, Pallas kernels, attention(): pl.pallas_call(attend_kernel, out_shape=(jax.ShapeDtypeStruct((own_rows,...  43.2 us
    unnamed x27, local copies, waits for them, and re-layouts  8.64 us

profile of v6, /device:TPU:38, one launch (start us, length us, event | category | flops | bytes accessed | tf_op | source)
XLA Modules:
  0.0 194.3 jit_solution(14771760031320923573)
XLA Ops:
  0.7 0.9 reduce-window.9
  1.6 0.7 bitcast_subtract_fusion
  2.3 0.1 convert_reduce_fusion
  2.4 0.1 select_reduce_fusion.1
  2.5 0.9 fusion.4
  3.4 1.2 fusion
  4.7 0.2 fusion.2.normed
  4.9 0.3 fusion.8
  5.3 0.3 subtract_convert_fusion
  5.6 0.2 pad_maximum_fusion.1
  5.8 0.3 copy-done.5
  6.1 0.3 convolution_convert_fusion
  6.5 0.8 copy-done.6
  7.3 0.1 pad_maximum_fusion.2
  7.4 0.1 copy.19.first
  7.6 0.7 copy-done.11
  8.2 0.2 select_reduce_fusion.blocks
  8.4 1.2 copy-done.2
  9.6 1.2 copy-done.3
  10.9 43.2 %attention.1 = (f32[16,2048]{1,0:T(8,128)S(1)}, bf16[8,16,256]{2,1,0:T(8,128)(2,1)S(1)}, bf16[8,16,256]{2,1,0:T(8,128)(2,1)S(1)}) custom-call(s32[8]{0:T(128)S(1)} %select_reduce_fusion.blocks, bf16[8,16,512]{2,1,0:T(8,128)(2,1)S(1)} %pad_maximum_fusion.mine, bf16[128,2048]{1,0:T(8,128)(2,1)S(1)} %fusion.2.normed, bf16[2048,256]{1,0:T(8,128)(2,1)S(1)} %copy-done.2, ...), custom_call_target="tpu_custom_call" | custom-call | tf_op jit(solution)/shard_map/attention/pallas_call | solution.py:235
  54.1 0.1 multiply_reduce_fusion
  54.3 0.4 copy-done.1
  54.7 0.4 copy-done.7
  55.0 0.3 fusion.7
  55.3 0.2 fusion.5
  55.5 0.5 copy-done.10
  56.2 0.1 fusion.3
  56.4 0.7 concatenate.24.mine
  57.1 134.1 %mixture.1 = bf16[8,16,2048]{2,1,0:T(8,128)(2,1)} custom-call(bf16[16,2176]{1,0:T(8,128)(2,1)} %concatenate.24.mine, f32[16,2048]{1,0:T(8,128)} %copy-done.1, bf16[2,2048,128]{2,1,0:T(8,128)(2,1)} %gate.1, bf16[2,2048,128]{2,1,0:T(8,128)(2,1)} %up_part.1, bf16[2,128,2048]{2,1,0:T(8,128)(2,1)} %down.1), custom_call_target="tpu_custom_call" | custom-call | tf_op jit(solution)/shard_map/mixture/pallas_call | solution.py:574
  191.2 1.9 copy.24
  193.0 0.6 copy.25
  193.7 0.6 copy.26
  (31 shorter events, 0.6 us)
Async XLA Ops:
  0.6 4.3 %copy-start = (bf16[2048,256]{1,0:T(8,128)(2,1)S(1)}, bf16[2048,256]{1,0:T(8,128)(2,1)}, u32[]{:S(2)}) copy-start(bf16[2048,256]{1,0:T(8,128)(2,1)} %param.19) | copy-start | bytes 3145732
  0.6 4.0 %copy-start.4 = (bf16[128,2048]{1,0:T(8,128)(2,1)S(1)}, bf16[128,2048]{1,0:T(8,128)(2,1)}, u32[]{:S(2)}) copy-start(bf16[128,2048]{1,0:T(8,128)(2,1)} %param.14) | copy-start | bytes 1572868
  3.4 1.3 copy-start.8
  4.9 1.2 copy-start.5
  6.4 0.8 copy-start.6
  7.5 0.7 copy-start.11
  8.4 1.2 copy-start.2
  9.6 1.2 copy-start.3
  10.8 43.3 %copy-start.9 = (f32[2048]{0:T(1024)S(1)}, f32[2048]{0:T(1024)}, u32[]{:S(2)}) copy-start(f32[2048]{0:T(1024)} %param.22) | copy-start | bytes 24580
  54.0 0.7 copy-start.1
  54.0 1.0 copy-start.7
  55.3 0.7 copy-start.10
